TPU v7x, 32 devices: a whole 2x2x4 slice. The times are simulated.
32 devices in a mesh: dp: 4 (over x, core), ctx: 2 (over y), tensor: 4 (over z).
Axes of the slice: x: 2, y: 2, z: 4, core: 2. Of those that a mesh axis runs over, the one named last changes fastest.
Arguments:
- tokens: bfloat16 [4, 1024, 768], P('dp', 'ctx'), may hold values from -24 to 24
- lengths: int32 [4], P('dp'), may hold values from 128 to 1024, as said below
- cotangent: bfloat16 [4, 1024, 768], P('dp', 'ctx'), may hold values from -6 to 6
- qkv_weight: bfloat16 [3, 768, 768], P(None, 'dp', 'tensor'), may hold values from -0.21875 to 0.21875
- query_bias: float32 [768], P('tensor'), may hold values from -3 to 3
- value_bias: float32 [768], P('tensor'), may hold values from -0.18 to 0.18
- proj_weight: bfloat16 [768, 768], P('tensor', 'dp'), may hold values from -6 to 6
- proj_bias: float32 [768], replicated, may hold values from -2 to 2
- first_gain: float32 [768], replicated, may hold values from 0.1 to 1.9
- first_shift: float32 [768], replicated, may hold values from -2 to 2
- up_weight: bfloat16 [768, 3072], P('dp', 'tensor'), may hold values from -0.21875 to 0.21875
- up_bias: float32 [3072], P('tensor'), may hold values from -2 to 2
- down_weight: bfloat16 [3072, 768], P('tensor', 'dp'), may hold values from -0.109375 to 0.109375
- down_bias: float32 [768], replicated, may hold values from -2 to 2
- second_gain: float32 [768], replicated, may hold values from 0.1 to 1.9
- second_shift: float32 [768], replicated, may hold values from -2 to 2
Outputs:
- output: bfloat16 [4, 1024, 768], P('dp', 'ctx')
- grad_tokens: float32 [4, 1024, 768], P('dp', 'ctx')
- grad_qkv: float32 [3, 768, 768], P(None, 'dp', 'tensor')
- grad_query_bias: float32 [768], P('tensor')
- grad_value_bias: float32 [768], P('tensor')
- grad_proj: float32 [768, 768], P('tensor', 'dp')
- grad_proj_bias: float32 [768], replicated
- grad_first_gain: float32 [768], replicated
- grad_first_shift: float32 [768], replicated
- grad_up: float32 [768, 3072], P('dp', 'tensor')
- grad_up_bias: float32 [3072], P('tensor')
- grad_down: float32 [3072, 768], P('tensor', 'dp')
- grad_down_bias: float32 [768], replicated
- grad_second_gain: float32 [768], replicated
- grad_second_shift: float32 [768], replicated
Inputs may be any that keep to these rules, and one draw needn't show every extreme that they name: `lengths`: positions at or beyond a sequence's length are padding; they are still computed, but no position attends to them.
All inputs are finite; a program needn't handle non-finite values.
Results may differ from a plain program's by a relative error of at most 0.013.
The roundings to bfloat16 on the way count: a program that leaves them out, or rounds other values in their place, can miss the bound.
Values may be sent and summed in bfloat16 or wider, within the bound.
A program may use at most 128 MiB of HBM per device.

v0:
```python
import functools
import math

import jax
import jax.numpy as jnp
from jax import lax
from jax.experimental import pallas as pl
from jax.experimental.pallas import tpu as pltpu
from jax.sharding import PartitionSpec as P

HD = 64


EPSILON = 1e-05
NEGATIVE = -1e30
ROOT_HALF = 0.7071067811865476
ROOT_TWO_PI = 2.5066282746310002
MESH = pl.DeviceIdType.MESH
BF16 = jnp.bfloat16
F32 = jnp.float32
VMEM_SPEC = pl.BlockSpec(memory_space=pltpu.VMEM)
DMA = pltpu.SemaphoreType.DMA


def layer_norm(hidden_in, norm_gain, norm_shift):
    centred = hidden_in - jnp.mean(hidden_in, axis=-1, keepdims=True)
    inverse = lax.rsqrt(jnp.mean(centred * centred, axis=-1, keepdims=True) + EPSILON)
    normed = centred * inverse
    return (normed * norm_gain + norm_shift, normed, inverse)


def norm_back(upstream, normed, inverse, norm_gain):
    scaled = upstream * norm_gain
    return inverse * (
        scaled
        - jnp.mean(scaled, axis=-1, keepdims=True)
        - normed * jnp.mean(scaled * normed, axis=-1, keepdims=True)
    )


def gelu_value(pre_act):
    return 0.5 * pre_act * (1.0 + jax.scipy.special.erf(pre_act * ROOT_HALF))


def gelu_slope(pre_act):
    return (
        0.5 * (1.0 + jax.scipy.special.erf(pre_act * ROOT_HALF))
        + pre_act * jnp.exp(-0.5 * pre_act * pre_act) / ROOT_TWO_PI
    )


def peers_of(axis, size):
    me = lax.axis_index(axis)
    found = []
    for step in range(1, size):
        other = lax.rem(me + step, size)
        found.append((other, {axis: other}))
    return found


def grid_peers(sizes):
    count = sizes["dp"] * sizes["ctx"]
    me = lax.axis_index("dp") * sizes["ctx"] + lax.axis_index("ctx")
    found = []
    for step in range(1, count):
        other = lax.rem(me + step, count)
        found.append((other, {"dp": lax.div(other, sizes["ctx"]), "ctx": lax.rem(other, sizes["ctx"])}))
    return me, found


def greet(groups):
    barrier = pltpu.get_barrier_semaphore()
    total = 0
    for group in groups:
        for _, where in group:
            pl.semaphore_signal(barrier, inc=1, device_id=where, device_id_type=MESH)
            total += 1
    pl.semaphore_wait(barrier, total)


def send_all(pairs, peers, send_sem, recv_sem):
    copies = []
    for step, (other, where) in enumerate(peers):
        source, target = pairs(other)
        copies.append(
            pltpu.make_async_remote_copy(
                src_ref=source,
                dst_ref=target,
                send_sem=send_sem.at[step],
                recv_sem=recv_sem.at[step],
                device_id=where,
                device_id_type=MESH,
            )
        )
        copies[-1].start()
    return copies


def wait_all(copies):
    for copy in copies:
        copy.wait()


def slot_sum(slots, count):
    total = slots[0].astype(F32)
    for index in range(1, count):
        total = total + slots[index].astype(F32)
    return total


def sems(count):
    return [DMA((count,)), DMA((count,))]


def call(kernel, outs, scratch, collective_id, args, name, spec=None):
    return pl.pallas_call(
        kernel,
        out_shape=outs,
        in_specs=[VMEM_SPEC] * len(args),
        out_specs=[VMEM_SPEC] * len(outs),
        scratch_shapes=scratch,
        compiler_params=pltpu.CompilerParams(
            collective_id=collective_id, has_side_effects=True, vmem_limit_bytes=56 * 2**20
        ),
        name=name,
    )(*args)


def shaped(shape, dtype):
    return jax.ShapeDtypeStruct(shape, dtype)


def pair_roles(size):
    me = lax.axis_index("dp")
    partner = me + 1 - 2 * lax.rem(me, 2)
    far = [(lax.rem(me + 2 * step, size), lax.rem(me + size - 2 * step, size)) for step in range(1, size // 2)]
    return me, partner, far


def pair_group(size):
    me, partner, far = pair_roles(size)
    return [(partner, {"dp": partner})] + [(to, {"dp": to}) for to, _ in far]


def remote(source, target, send, recv, where):
    return pltpu.make_async_remote_copy(
        src_ref=source, dst_ref=target, send_sem=send, recv_sem=recv, device_id=where, device_id_type=MESH
    )


def pair_sems(size):
    return sems(1) + sems(max(1, size // 2 - 1)) * 2


def gather_start(size, own_ref, place, sem):
    me, partner, far = pair_roles(size)
    near = remote(own_ref, place(me), sem[0].at[0], sem[1].at[0], {"dp": partner})
    wide = [
        remote(own_ref, place(me), sem[2].at[step], sem[3].at[step], {"dp": to})
        for step, (to, _) in enumerate(far)
    ]
    for copy in wide + [near]:
        copy.start()
    return near, wide


def gather_pass(size, copies, place, sem):
    me, partner, far = pair_roles(size)
    passed = []
    for step, (_, origin) in enumerate(far):
        copies[1][step].wait()
        passed.append(
            remote(place(origin), place(origin), sem[4].at[step], sem[5].at[step], {"dp": partner})
        )
        passed[-1].start()
    return [copies[0]] + passed


def gather_kernel(sizes, qkv_ref, wide_qkv, *sem):
    size = sizes["dp"]
    greet([pair_group(size)])
    place = lambda index: wide_qkv.at[:, index]
    copies = gather_start(size, qkv_ref, place, sem)
    wide_qkv[:, lax.axis_index("dp")] = qkv_ref[...]
    wait_all(gather_pass(size, copies, place, sem))


def ctx_gather_kernel(sizes, own_ref, proj_ref, wide, wide_proj, *sem):
    me = lax.axis_index("ctx")
    size = sizes["dp"]
    peers = peers_of("ctx", sizes["ctx"])
    greet([peers, pair_group(size)])
    copies = send_all(lambda other: (own_ref, wide.at[me]), peers, sem[0], sem[1])
    place = lambda index: wide_proj.at[index]
    projs = gather_start(size, proj_ref, place, sem[2:])
    wide[me] = own_ref[...]
    wide_proj[lax.axis_index("dp")] = proj_ref[...]
    wait_all(gather_pass(size, projs, place, sem[2:]))
    wait_all(copies)


LAG = 4
CHUNK = 32


def line_roles(size):
    me = lax.axis_index("tensor")
    lower, upper = lax.rem(me + size - 1, size), lax.rem(me + 1, size)
    return [(me, lower, upper), (size - 1 - me, upper, lower)]


def greet_line(size, groups):
    me = lax.axis_index("tensor")
    barrier = pltpu.get_barrier_semaphore()

    @pl.when(me > 0)
    def _():
        pl.semaphore_signal(barrier, inc=1, device_id={"tensor": me - 1}, device_id_type=MESH)

    @pl.when(me < size - 1)
    def _():
        pl.semaphore_signal(barrier, inc=1, device_id={"tensor": me + 1}, device_id_type=MESH)

    total = 0
    for group in groups:
        for _, where in group:
            pl.semaphore_signal(barrier, inc=1, device_id=where, device_id_type=MESH)
            total += 1

    beside = jnp.where(me > 0, 1, 0) + jnp.where(me < size - 1, 1, 0)
    pl.semaphore_wait(barrier, total + beside)


def both(*conditions):
    return functools.reduce(jnp.logical_and, conditions)


def line_start(size, part, slots, sem):
    count = part.shape[1]
    for flow, (place, toward, _) in enumerate(line_roles(size)):

        @pl.when(place == size - 1)
        def _(flow=flow, toward=toward):
            @pl.loop(0, count)
            def _(k):
                remote(
                    part.at[flow, k], slots.at[flow, k], sem[0].at[flow, k], sem[1].at[flow, k], {"tensor": toward}
                ).start()


def line_run(size, part, slots, sums, full, sem, finish, between=()):
    count = part.shape[1]
    roles = line_roles(size)

    def reduce_copy(flow, k, source):
        return remote(
            source.at[flow, k], slots.at[flow, k], sem[0].at[flow, k], sem[1].at[flow, k], {"tensor": roles[flow][1]}
        )

    def spread_copy(flow, k):
        return remote(
            full.at[flow, k], full.at[flow, k], sem[2].at[flow, k], sem[3].at[flow, k], {"tensor": roles[flow][2]}
        )

    def one_step(step):
        for flow, (place, _, _) in enumerate(roles):
            k = step - LAG * (size - 1 - place)
            inside = both(k >= 0, k < count)

            @pl.when(both(inside, place > 0, place < size - 1))
            def _(flow=flow, k=k):
                reduce_copy(flow, k, sums).wait_recv()
                sums[flow, k] = (slots[flow, k].astype(F32) + part[flow, k].astype(F32)).astype(BF16)
                reduce_copy(flow, k, sums).start()

            @pl.when(both(inside, place == 0))
            def _(flow=flow, k=k):
                reduce_copy(flow, k, sums).wait_recv()
                full[flow, k] = finish(flow, k, slots[flow, k].astype(F32) + part[flow, k].astype(F32))
                spread_copy(flow, k).start()

        for flow, (place, _, _) in enumerate(roles):
            k = step - LAG * (size - 1) - LAG * place
            inside = both(k >= 0, k < count, place > 0)

            @pl.when(inside)
            def _(flow=flow, k=k):
                spread_copy(flow, k).wait_recv()

            @pl.when(both(inside, place < size - 1))
            def _(flow=flow, k=k):
                spread_copy(flow, k).start()

    begun, last = 0, count + 2 * LAG * (size - 1)
    for stop, action in tuple(between) + ((last, None),):
        stop = min(stop, last)
        pl.loop(begun, stop)(one_step)
        begun = stop
        if action is not None:
            action()

    for flow, (place, _, _) in enumerate(roles):

        @pl.when(place > 0)
        def _(flow=flow):
            @pl.loop(0, count)
            def _(k):
                reduce_copy(flow, k, sums).wait_send()

        @pl.when(place < size - 1)
        def _(flow=flow):
            @pl.loop(0, count)
            def _(k):
                spread_copy(flow, k).wait_send()


def spread_start(size, mine, full, sem):
    for flow, (place, _, away) in enumerate(line_roles(size)):

        @pl.when(place == 0)
        def _(flow=flow, away=away):
            @pl.loop(0, mine.shape[0])
            def _(k):
                remote(
                    mine.at[k], full.at[flow, k], sem[0].at[flow, k], sem[1].at[flow, k], {"tensor": away}
                ).start()
                full[flow, k] = mine[k]


def spread_run(size, mine, full, sem):
    count = mine.shape[0]
    roles = line_roles(size)

    def pass_on(flow, k):
        return remote(
            full.at[flow, k], full.at[flow, k], sem[0].at[flow, k], sem[1].at[flow, k], {"tensor": roles[flow][2]}
        )

    @pl.loop(0, count + LAG * (size - 1))
    def _(step):
        for flow, (place, _, _) in enumerate(roles):
            k = step - LAG * place
            inside = both(k >= 0, k < count, place > 0)

            @pl.when(inside)
            def _(flow=flow, k=k):
                pass_on(flow, k).wait_recv()

            @pl.when(both(inside, place < size - 1))
            def _(flow=flow, k=k):
                pass_on(flow, k).start()

    for flow, (place, _, _) in enumerate(roles):

        @pl.when(place < size - 1)
        def _(flow=flow):
            @pl.loop(0, count)
            def _(k):
                pass_on(flow, k).wait_send()


def line_sems(count, kinds):
    return [DMA((2, count))] * kinds


def ctx_sum_kernel(sizes, part_ref, mine, total_ref, full, slots, *sem):
    me = lax.axis_index("ctx")
    size = sizes["tensor"]
    peers = peers_of("ctx", sizes["ctx"])
    greet_line(size, [peers])
    copies = send_all(lambda other: (part_ref.at[other], slots.at[me]), peers, sem[0], sem[1])
    spread_start(size, mine, full, sem[2:4])
    slots[me] = part_ref[me]
    spread_run(size, mine, full, sem[2:4])
    wait_all(copies)
    total_ref[...] = slot_sum(slots, sizes["ctx"])


def first_kernel(
    sizes, part, tokens, fixed, up, down,
    full, out_ref, normed_ref, inverse_ref, wide_up, wide_down,
    slots, sums, *sem
):
    size, data = sizes["tensor"], sizes["dp"]
    mine = lax.axis_index("dp")
    greet_line(size, [pair_group(data)])
    line_start(size, part, slots, sem[0:2])
    place_up, place_down = (lambda index: wide_up.at[index]), (lambda index: wide_down.at[index])
    ups = gather_start(data, up, place_up, sem[4:10])
    downs = gather_start(data, down, place_down, sem[10:16])
    wide_up[mine] = up[...]
    wide_down[mine] = down[...]

    def finish(flow, k, total):
        first_sum = tokens[flow, k].astype(F32) + total + fixed[0:1]
        first_out, normed, inverse = layer_norm(first_sum, fixed[1:2], fixed[2:3])
        out_ref[k] = first_out
        normed_ref[k] = normed
        inverse_ref[k] = inverse
        return first_out.astype(BF16)

    passed = []

    def hand_over():
        passed.extend(gather_pass(data, ups, place_up, sem[4:10]))
        passed.extend(gather_pass(data, downs, place_down, sem[10:16]))

    line_run(size, part, slots, sums, full, sem[0:4], finish, [(LAG * size, hand_over)])
    wait_all(passed)


def add_row(vector_ref, index, value):
    vector_ref[index : index + 1] += jnp.sum(value, axis=0, keepdims=True)


def second_kernel(
    sizes, part, first_out, cotangent, fixed,
    full, output_ref, back_ref, vector_ref,
    slots, sums, *sem
):
    size = sizes["tensor"]
    greet_line(size, [])
    line_start(size, part, slots, sem[0:2])
    vector_ref[...] = jnp.zeros_like(vector_ref)

    def finish(flow, k, total):
        second_sum = first_out[k] + total + fixed[3:4]
        result, normed, inverse = layer_norm(second_sum, fixed[4:5], fixed[5:6])
        upstream = cotangent[flow, k].astype(F32)
        d_second = norm_back(upstream, normed, inverse, fixed[4:5])
        output_ref[k] = result.astype(BF16)
        back_ref[k] = d_second
        add_row(vector_ref, 0, upstream)
        add_row(vector_ref, 1, upstream * normed)
        add_row(vector_ref, 2, d_second)
        return d_second.astype(BF16)

    line_run(size, part, slots, sums, full, sem[0:4], finish)


def grads_start(size, grads, chip, sem):
    me, partner, _ = pair_roles(size)
    copy = remote(
        grads.at[:, lax.rem(partner, 2)], chip, sem[0].at[0], sem[1].at[0], {"dp": partner}
    )
    copy.start()
    return copy


def grads_far(size, copy, grads, chip, merged, slots, sem):
    me, _, far = pair_roles(size)
    copy.wait()
    merged[...] = (grads[:, lax.rem(me, 2)].astype(F32) + chip[...].astype(F32)).astype(BF16)
    copies = [
        remote(
            merged.at[lax.div(to, 2)], slots.at[lax.div(me, 2)], sem[2].at[step], sem[3].at[step], {"dp": to}
        )
        for step, (to, _) in enumerate(far)
    ]
    for moving in copies:
        moving.start()
    slots[lax.div(me, 2)] = merged[lax.div(me, 2)]
    return copies


def blocks_start(sizes, value, blocks, sem):
    me = lax.axis_index("ctx")
    blocks[me] = value
    return send_all(
        lambda other: (blocks.at[me], blocks.at[me]), peers_of("ctx", sizes["ctx"]), sem[0], sem[1]
    )


def third_kernel(
    sizes, part, d_second, normed_ref, inverse_ref, fixed, grads_a, grads_b,
    full, back_ref, vector_ref, block_a, block_b,
    slots, sums, chip_a, chip_b, merged_a, merged_b, far_a, far_b, *sem
):
    size, data = sizes["tensor"], sizes["dp"]
    greet_line(size, [pair_group(data)])
    line_start(size, part, slots, sem[0:2])
    near_a = grads_start(data, grads_a, chip_a, sem[4:8])
    near_b = grads_start(data, grads_b, chip_b, sem[8:12])
    vector_ref[...] = jnp.zeros_like(vector_ref)
    moving_a, moving_b = [], []

    def go_far():
        moving_a.extend(grads_far(data, near_a, grads_a, chip_a, merged_a, far_a, sem[4:8]))
        moving_b.extend(grads_far(data, near_b, grads_b, chip_b, merged_b, far_b, sem[8:12]))

    def finish(flow, k, total):
        d_first = total + d_second[k]
        normed = normed_ref[k]
        d_attn = norm_back(d_first, normed, inverse_ref[k], fixed[1:2])
        back_ref[k] = d_attn
        add_row(vector_ref, 0, d_first)
        add_row(vector_ref, 1, d_first * normed)
        add_row(vector_ref, 2, d_attn)
        return d_attn.astype(BF16)

    line_run(size, part, slots, sums, full, sem[0:4], finish, [(LAG, go_far)])
    wait_all(moving_a)
    block_a[...] = slot_sum(far_a, data // 2).astype(BF16)
    wait_all(moving_b)
    block_b[...] = slot_sum(far_b, data // 2).astype(BF16)


def last_kernel(
    sizes, part, d_attn, grads, block_a, block_b, vectors,
    full, owned, owned_a, owned_b, vector_ref,
    slots, sums, chip, merged, far, blocks, blocks_a, blocks_b, slots_v, grid_v, *sem
):
    size, data = sizes["tensor"], sizes["dp"]
    me = lax.axis_index("tensor")
    rows = peers_of("tensor", size)
    here, everyone = grid_peers(sizes)
    greet([rows, everyone])
    line_start(size, part, slots, sem[0:2])
    small = send_all(lambda other: (vectors, slots_v.at[me]), rows, sem[8], sem[9])
    near = grads_start(data, grads, chip, sem[4:8])
    moving_a = blocks_start(sizes, block_a[...], blocks_a, sem[12:14])
    moving_b = blocks_start(sizes, block_b[...], blocks_b, sem[14:16])
    slots_v[me] = vectors[...]
    state = {}

    def go_far():
        state["far"] = grads_far(data, near, grads, chip, merged, far, sem[4:8])
        wait_all(small)
        own = vectors[...]
        row_ids = lax.broadcasted_iota(jnp.int32, own.shape, 0)
        grid_v[here] = jnp.where(row_ids < 6, slot_sum(slots_v, size), own)
        state["small"] = send_all(
            lambda other: (grid_v.at[here], grid_v.at[here]), everyone, sem[10], sem[11]
        )

    def go_across():
        wait_all(state["far"])
        value = slot_sum(far, data // 2).astype(BF16)
        state["across"] = blocks_start(sizes, value, blocks, sem[16:18])

    def finish(flow, k, total):
        return (total + d_attn[k]).astype(BF16)

    between = [(LAG, go_far), (LAG * size, go_across)]
    line_run(size, part, slots, sums, full, sem[0:4], finish, between)
    wait_all(state["small"])
    vector_ref[...] = slot_sum(grid_v, data * sizes["ctx"])
    wait_all(moving_a)
    owned_a[...] = slot_sum(blocks_a, sizes["ctx"])
    wait_all(moving_b)
    owned_b[...] = slot_sum(blocks_b, sizes["ctx"])
    wait_all(state["across"])
    owned[...] = slot_sum(blocks, sizes["ctx"])


CONTRACT_LAST = (((1,), (1,)), ((), ()))
CONTRACT_FIRST = (((0,), (0,)), ((), ()))


def forward_kernel(score_scale, length_ref, q_ref, k_ref, v_ref, out_ref, low_ref, log_ref):
    length = length_ref[0]
    rows, width = q_ref.shape
    keys = k_ref.shape[0]
    block = math.gcd(rows, 256)
    valid = lax.broadcasted_iota(jnp.int32, (block, keys), 1) < length

    @pl.loop(0, rows // block)
    def _(step):
        here = pl.ds(pl.multiple_of(step * block, block), block)
        for head in range(width // HD):
            lanes = slice(head * HD, (head + 1) * HD)
            scores = lax.dot_general(
                q_ref[here, lanes], k_ref[:, lanes], CONTRACT_LAST, preferred_element_type=F32
            ) * score_scale
            scores = jnp.where(valid, scores, NEGATIVE)
            top = jnp.max(scores, axis=-1, keepdims=True)
            weights = jnp.where(valid, jnp.exp(scores - top), 0.0)
            total = jnp.sum(weights, axis=-1, keepdims=True)
            acc = jnp.dot(weights.astype(BF16), v_ref[:, lanes], preferred_element_type=F32)
            attended = acc / total
            out_ref[here, lanes] = attended
            low_ref[here, lanes] = attended.astype(BF16)
            log_ref[here, head : head + 1] = top + jnp.log(total)


def backward_kernel(
    score_scale, length_ref, q_ref, k_ref, v_ref, heads_ref, attended_ref, log_ref,
    dq_ref, dk_ref, dv_ref
):
    length = length_ref[0]
    rows, width = q_ref.shape
    keys = k_ref.shape[0]
    block = math.gcd(rows, 256)
    valid = lax.broadcasted_iota(jnp.int32, (block, keys), 1) < length
    dk_ref[...] = jnp.zeros_like(dk_ref)
    dv_ref[...] = jnp.zeros_like(dv_ref)

    @pl.loop(0, rows // block)
    def _(step):
        here = pl.ds(pl.multiple_of(step * block, block), block)
        for head in range(width // HD):
            lanes = slice(head * HD, (head + 1) * HD)
            q, k, v, d_heads = q_ref[here, lanes], k_ref[:, lanes], v_ref[:, lanes], heads_ref[here, lanes]
            delta = jnp.sum(d_heads.astype(F32) * attended_ref[here, lanes], axis=-1, keepdims=True)
            scores = lax.dot_general(q, k, CONTRACT_LAST, preferred_element_type=F32) * score_scale
            scores = jnp.where(valid, scores, NEGATIVE)
            probs = jnp.where(valid, jnp.exp(scores - log_ref[here, head : head + 1]), 0.0)
            d_probs = lax.dot_general(d_heads, v, CONTRACT_LAST, preferred_element_type=F32)
            d_scores = (probs * (d_probs - delta)).astype(BF16)
            dv_ref[:, lanes] += lax.dot_general(
                probs.astype(BF16), d_heads, CONTRACT_FIRST, preferred_element_type=F32
            )
            dk_ref[:, lanes] += lax.dot_general(
                d_scores, q, CONTRACT_FIRST, preferred_element_type=F32
            ) * score_scale
            dq_ref[here, lanes] = jnp.dot(d_scores, k, preferred_element_type=F32) * score_scale


def attention_call(kernel, outs, args, name):
    return pl.pallas_call(
        kernel,
        out_shape=outs,
        in_specs=[pl.BlockSpec(memory_space=pltpu.SMEM)] + [VMEM_SPEC] * (len(args) - 1),
        out_specs=[VMEM_SPEC] * len(outs),
        compiler_params=pltpu.CompilerParams(vmem_limit_bytes=56 * 2**20),
        name=name,
    )(*args)


def per_device(
    sizes,
    tokens,
    lengths,
    cotangent,
    qkv_weight,
    query_bias,
    value_bias,
    proj_weight,
    proj_bias,
    first_gain,
    first_shift,
    up_weight,
    up_bias,
    down_weight,
    down_bias,
    second_gain,
    second_shift,
):
    data, blocks, ranks = sizes["dp"], sizes["ctx"], sizes["tensor"]
    rows_in = tokens[0]
    row_count, model = rows_in.shape
    half = row_count // 2
    chunk = math.gcd(half, CHUNK)
    chunks = half // chunk
    piece, local_width = qkv_weight.shape[1:]
    up_width = up_weight.shape[1]
    score_scale = 1.0 / math.sqrt(HD)
    split = (2, chunks, chunk, model)
    line_scratch = [pltpu.VMEM(split, BF16)] * 2 + line_sems(chunks, 4)
    local = shaped(split[1:], F32)
    fixed = jnp.zeros((8, model), F32)
    row_ids = lax.broadcasted_iota(jnp.int32, fixed.shape, 0)
    for index, vector in enumerate(
        [proj_bias, first_gain, first_shift, down_bias, second_gain, second_shift]
    ):
        fixed = jnp.where(row_ids == index, vector[None], fixed)

    (wide_qkv,) = call(
        functools.partial(gather_kernel, sizes),
        [shaped((3, data, piece, local_width), BF16)],
        pair_sems(data),
        0,
        (qkv_weight,),
        "gather_weights",
    )
    wide_qkv = wide_qkv.reshape(3, model, local_width)

    projected = jnp.einsum("td,ide->ite", rows_in, wide_qkv, preferred_element_type=F32)
    queries = (projected[0] + query_bias).astype(BF16)
    own_kv = jnp.concatenate(
        [projected[1].astype(BF16), (projected[2] + value_bias).astype(BF16)], axis=1
    )
    kv, wide_proj = call(
        functools.partial(ctx_gather_kernel, sizes),
        [shaped((blocks,) + own_kv.shape, BF16), shaped((data,) + proj_weight.shape, BF16)],
        sems(blocks - 1) + pair_sems(data),
        1,
        (own_kv, proj_weight),
        "gather_keys",
    )
    wide_proj = wide_proj.transpose(1, 0, 2).reshape(local_width, model)
    kv = kv.reshape(blocks * row_count, 2 * local_width)
    keys, values = kv[:, :local_width], kv[:, local_width:]
    attended, attended_low, log_total = attention_call(
        functools.partial(forward_kernel, score_scale),
        [
            shaped((row_count, local_width), F32),
            shaped((row_count, local_width), BF16),
            shaped((row_count, local_width // HD), F32),
        ],
        (lengths, queries, keys, values),
        "attention_forward",
    )
    attn_part = jnp.dot(attended_low, wide_proj, preferred_element_type=F32).astype(BF16)

    first_low, first_out, first_normed, first_inverse, wide_up, wide_down = call(
        functools.partial(first_kernel, sizes),
        [
            shaped(split, BF16),
            local,
            local,
            shaped((chunks, chunk, 1), F32),
            shaped((data,) + up_weight.shape, BF16),
            shaped((data,) + down_weight.shape, BF16),
        ],
        line_scratch + pair_sems(data) * 2,
        2,
        (
            attn_part.reshape(split),
            rows_in.reshape(split),
            fixed,
            up_weight,
            down_weight,
        ),
        "first_norm",
    )
    first_low = first_low.reshape(row_count, model)
    wide_up = wide_up.reshape(model, up_width)
    wide_down = wide_down.transpose(1, 0, 2).reshape(up_width, model)

    pre_act = jnp.dot(first_low, wide_up, preferred_element_type=F32) + up_bias
    hidden = gelu_value(pre_act).astype(BF16)
    down_part = jnp.dot(hidden, wide_down, preferred_element_type=F32).astype(BF16)
    d_second_low, output_part, d_second, second_vectors = call(
        functools.partial(second_kernel, sizes),
        [shaped(split, BF16), shaped(split[1:], BF16), local, shaped((3, model), F32)],
        line_scratch,
        3,
        (
            down_part.reshape(split),
            first_out,
            cotangent[0].reshape(split),
            fixed,
        ),
        "second_norm",
    )
    d_second_low = d_second_low.reshape(row_count, model)
    grad_down = jnp.einsum("td,tf->df", d_second_low, hidden, preferred_element_type=F32)
    d_hidden = jnp.einsum("td,fd->tf", d_second_low, wide_down, preferred_element_type=F32)
    d_pre = d_hidden * gelu_slope(pre_act)
    grad_up_bias = jnp.sum(d_pre, axis=0)
    d_pre_low = d_pre.astype(BF16)
    grad_up = jnp.einsum("td,tf->df", first_low, d_pre_low, preferred_element_type=F32)
    first_part = jnp.einsum("tf,df->td", d_pre_low, wide_up, preferred_element_type=F32).astype(BF16)

    grad_shape = (data, model // data, up_width)
    paired = (data // 2, 2) + grad_shape[1:]
    pair_slots = pltpu.VMEM((data // 2,) + grad_shape[1:], BF16)
    pair_moves = sems(1) + sems(max(1, data // 2 - 1))
    d_attn_low, d_attn, first_vectors, block_up, block_down = call(
        functools.partial(third_kernel, sizes),
        [shaped(split, BF16), local, shaped((3, model), F32)] + [shaped(grad_shape[1:], BF16)] * 2,
        line_scratch[:2] + [pair_slots] * 6 + line_scratch[2:] + pair_moves * 2,
        4,
        (
            first_part.reshape(split),
            d_second,
            first_normed,
            first_inverse,
            fixed,
            grad_up.astype(BF16).reshape(paired),
            grad_down.astype(BF16).reshape(paired),
        ),
        "first_norm_back",
    )
    d_attn_low = d_attn_low.reshape(row_count, model)
    d_heads = jnp.einsum("td,ed->te", d_attn_low, wide_proj, preferred_element_type=F32).astype(BF16)
    d_query, key_grads, value_grads = attention_call(
        functools.partial(backward_kernel, score_scale),
        [shaped((row_count, local_width), F32)]
        + [shaped((blocks * row_count, local_width), F32)] * 2,
        (lengths, queries, keys, values, d_heads, attended, log_total),
        "attention_backward",
    )
    kv_part = jnp.concatenate([key_grads.astype(BF16), value_grads.astype(BF16)], axis=1)
    kv_shape = (blocks, row_count, 2 * local_width)
    own_grads, output = call(
        functools.partial(ctx_sum_kernel, sizes),
        [shaped(kv_shape[1:], F32), shaped(split, BF16)],
        [pltpu.VMEM(kv_shape, BF16)] + sems(blocks - 1) + line_sems(chunks, 2),
        5,
        (kv_part.reshape(kv_shape), output_part),
        "sum_keys",
    )
    grad_query_bias = jnp.sum(d_query, axis=0)
    grad_value_bias = jnp.sum(own_grads[:, local_width:], axis=0)
    d_stack = jnp.concatenate([d_query.astype(BF16), own_grads.astype(BF16)], axis=1)
    grad_qkv = jnp.einsum("td,te->de", rows_in, d_stack, preferred_element_type=F32)
    grad_proj = jnp.einsum("td,te->de", d_attn_low, attended_low, preferred_element_type=F32)
    flat_qkv = wide_qkv.transpose(1, 0, 2).reshape(model, 3 * local_width)
    input_part = jnp.einsum("te,de->td", d_stack, flat_qkv, preferred_element_type=F32).astype(BF16)

    last_shape = (data // 2, 2, model // data, 4 * local_width)
    last_pair = pltpu.VMEM((data // 2,) + last_shape[2:], BF16)
    last_grads = jnp.concatenate([grad_qkv.astype(BF16), grad_proj.astype(BF16)], axis=1)
    vector_width = max(model, up_width, 2 * local_width)
    pad = lambda array: jnp.pad(array, ((0, 0), (0, vector_width - array.shape[1])))
    vectors = jnp.concatenate(
        [
            pad(second_vectors),
            pad(first_vectors),
            pad(grad_up_bias[None]),
            pad(jnp.concatenate([grad_query_bias, grad_value_bias])[None]),
        ]
    )
    grad_tokens, own_last, own_up, own_down, sums = call(
        functools.partial(last_kernel, sizes),
        [shaped(split, BF16), shaped(last_shape[2:], F32)]
        + [shaped(grad_shape[1:], F32)] * 2
        + [shaped(vectors.shape, F32)],
        line_scratch[:2]
        + [last_pair] * 3
        + [pltpu.VMEM((blocks,) + last_shape[2:], BF16)]
        + [pltpu.VMEM((blocks,) + grad_shape[1:], BF16)] * 2
        + [
            pltpu.VMEM((ranks,) + vectors.shape, F32),
            pltpu.VMEM((data * blocks,) + vectors.shape, F32),
        ]
        + line_scratch[2:]
        + pair_moves
        + sems(ranks - 1)
        + sems(data * blocks - 1)
        + sems(blocks - 1) * 3,
        6,
        (
            input_part.reshape(split),
            d_attn,
            last_grads.reshape(last_shape),
            block_up,
            block_down,
            vectors,
        ),
        "token_grads",
    )
    grad_tokens = grad_tokens.reshape(1, row_count, model).astype(F32)
    own_qkv = own_last[:, : 3 * local_width].reshape(-1, 3, local_width).transpose(1, 0, 2)
    return (
        output.reshape(1, row_count, model),
        grad_tokens,
        own_qkv,
        sums[7, :local_width],
        sums[7, local_width : 2 * local_width],
        own_last[:, 3 * local_width :].T,
        sums[5, :model],
        sums[4, :model],
        sums[3, :model],
        own_up,
        sums[6, :up_width],
        own_down.T,
        sums[2, :model],
        sums[1, :model],
        sums[0, :model],
    )


def solution(mesh):
    placed = (
        P("dp", "ctx", None),
        P("dp"),
        P("dp", "ctx", None),
        P(None, "dp", "tensor"),
        P("tensor"),
        P("tensor"),
        P("tensor", "dp"),
        P(),
        P(),
        P(),
        P("dp", "tensor"),
        P("tensor"),
        P("tensor", "dp"),
        P(),
        P(),
        P(),
    )
    return jax.shard_map(
        functools.partial(per_device, dict(mesh.shape)),
        mesh=mesh,
        in_specs=placed,
        out_specs=(
            P("dp", "ctx", None),
            P("dp", "ctx", None),
            P(None, "dp", "tensor"),
            P("tensor"),
            P("tensor"),
            P("tensor", "dp"),
            P(),
            P(),
            P(),
            P("dp", "tensor"),
            P("tensor"),
            P("tensor", "dp"),
            P(),
            P(),
            P(),
        ),
        check_vma=False,
    )
```

profile of v0, /device:TPU:0, one launch (start us, length us, event | category | flops | bytes accessed | tf_op | source)
XLA Modules:
  0.0 253.8 jit_solution(13434424702905180740)
XLA Ops:
  1.3 1.5 select_select_fusion.fixed
  2.8 1.9 copy.52.down
  4.7 14.0 %gather_weights.1 = bf16[3,4,192,192]{3,2,1,0:T(8,128)(2,1)} custom-call(bf16[3,192,192]{2,1,0:T(8,128)(2,1)} %qkv_ref.1), custom_call_target="tpu_custom_call" | custom-call | tf_op jit(solution)/shard_map/gather_weights/pallas_call | solution.py:116
  18.6 1.8 copy.55
  23.0 14.1 %gather_keys.1 = (bf16[2,512,384]{2,1,0:T(8,128)(2,1)}, bf16[4,192,192]{2,1,0:T(8,128)(2,1)}) custom-call(bf16[512,384]{1,0:T(8,128)(2,1)} %pad_maximum_fusion.5.own_ref, bf16[192,192]{1,0:T(8,128)(2,1)} %proj_ref.1), custom_call_target="tpu_custom_call" | custom-call | tf_op jit(solution)/shard_map/gather_keys/pallas_call | solution.py:116
  40.0 5.6 %attention_forward.1 = (f32[512,192]{1,0:T(8,128)}, bf16[512,192]{1,0:T(8,128)(2,1)}, f32[512,3]{1,0:T(8,128)}) custom-call(s32[1]{0:T(128)S(6)} %copy.65.length_ref, bf16[512,192]{1,0:T(8,128)(2,1)} %get-tuple-element.128.q_ref, bf16[1024,192]{1,0:T(8,128)(2,1)} %get-tuple-element.130.k_ref, bf16[1024,192]{1,0:T(8,128)(2,1)} %get-tuple-element.129.v_ref), custom_call_target="tpu_custom_call" | custom-call | tf_op jit(solution)/shard_map/attention_forward/pallas_call | solution.py:620
  45.6 2.2 convolution_convert_fusion.6
  47.8 35.4 %first_norm.1 = (bf16[2,8,32,768]{3,2,1,0:T(8,128)(2,1)}, f32[8,32,768]{2,1,0:T(8,128)}, f32[8,32,768]{2,1,0:T(8,128)}, f32[8,32,1]{2,1,0:T(8,128)}, bf16[4,192,...) custom-call(bf16[2,8,32,768]{3,2,1,0:T(8,128)(2,1)} %bitcast.83, bf16[2,8,32,768]{3,2,1,0:T(8,128)(2,1)} %bitcast.93, ...), custom_call_target="tpu_custom_call" | custom-call | tf_op jit(solution)/shard_map/first_norm/pallas_call | solution.py:116
  83.2 1.8 copy.53
  85.0 2.0 multiply_convert_fusion
  87.1 1.7 convolution_convert_fusion.4
  88.7 30.5 %second_norm.1 = (bf16[2,8,32,768]{3,2,1,0:T(8,128)(2,1)}, bf16[8,32,768]{2,1,0:T(8,128)(2,1)}, f32[8,32,768]{2,1,0:T(8,128)}, f32[3,768]{1,0:T(4,128)}) custom-call(bf16[2,8,32,768]{3,2,1,0:T(8,128)(2,1)} %bitcast.98, f32[8,32,768]{2,1,0:T(8,128)} %get-tuple-element.51.first_out, bf16[2,8,32,768]{3,2,1,0:T(8,128)(2,1)} %bitcast.95, ...), custom_call_target="tpu_custom_call" | custom-call | tf_op jit(solution)/shard_map/second_norm/pallas_call | solution.py:116
  119.3 2.3 fusion.20
  121.5 1.8 convolution_convert_fusion
  123.4 1.7 convolution_convert_fusion.3
  125.1 1.8 convolution_convert_fusion.1
  126.9 32.9 %first_norm_back.1 = (bf16[2,8,32,768]{3,2,1,0:T(8,128)(2,1)}, f32[8,32,768]{2,1,0:T(8,128)}, f32[3,768]{1,0:T(4,128)}, bf16[192,768]{1,0:T(8,128)(2,1)}, bf16[192,768]{1,0:T(8,128)(2,1)}) custom-call(bf16[2,8,32,768]{3,2,1,0:T(8,128)(2,1)} %bitcast.92, f32[8,32,768]{2,1,0:T(8,128)} %get-tuple-element.53.d_second, ...), custom_call_target="tpu_custom_call" | custom-call | tf_op jit(solution)/shard_map/first_norm_back/pallas_call | solution.py:116
  159.8 1.5 convolution_convert_fusion.8
  161.3 1.5 convolution_convert_fusion.7
  163.7 8.6 %attention_backward.1 = (f32[512,192]{1,0:T(8,128)}, f32[1024,192]{1,0:T(8,128)}, f32[1024,192]{1,0:T(8,128)}) custom-call(s32[1]{0:T(128)S(6)} %copy.65.length_ref, bf16[512,192]{1,0:T(8,128)(2,1)} %get-tuple-element.128.q_ref, bf16[1024,192]{1,0:T(8,128)(2,1)} %get-tuple-element.130.k_ref, bf16[1024,192]{1,0:T(8,128)(2,1)} %get-tuple-element.129.v_ref, ...), custom_call_target="tpu_custom_call" | custom-call | tf_op jit(solution)/shard_map/attention_backward/pallas_call | solution.py:620
  175.3 19.1 %sum_keys.1 = (f32[512,384]{1,0:T(8,128)}, bf16[2,8,32,768]{3,2,1,0:T(8,128)(2,1)}) custom-call(bf16[2,512,384]{2,1,0:T(8,128)(2,1)} %bitcast.80, bf16[8,32,768]{2,1,0:T(8,128)(2,1)} %get-tuple-element.61.mine), custom_call_target="tpu_custom_call" | custom-call | tf_op jit(solution)/shard_map/sum_keys/pallas_call | solution.py:116
  196.8 1.7 convolution_convert_fusion.5
  201.7 41.1 %token_grads.1 = (bf16[2,8,32,768]{3,2,1,0:T(8,128)(2,1)}, f32[192,768]{1,0:T(8,128)}, f32[192,768]{1,0:T(8,128)}, f32[192,768]{1,0:T(8,128)}, f32[8,768]{1,0:T(8,128)}) custom-call(bf16[2,8,32,768]{3,2,1,0:T(8,128)(2,1)} %bitcast.97, f32[8,32,768]{2,1,0:T(8,128)} %get-tuple-element.65.d_attn, bf16[2,2,192,768]{3,2,1,0:T(8,128)(2,1)} %bitcast.77, ...), custom_call_target="tpu_custom_call" | custom-call | tf_op jit(solution)/shard_map/token_grads/pallas_call | solution.py:116
  244.2 1.7 slice_reduce_fusion.1
  (72 shorter events, 24.2 us)
Async XLA Ops:
  4.7 15.8 %copy-start.4 = (bf16[1,512,768]{2,1,0:T(8,128)(2,1)S(1)}, bf16[1,512,768]{2,1,0:T(8,128)(2,1)}, u32[]{:S(2)}) copy-start(bf16[1,512,768]{2,1,0:T(8,128)(2,1)} %param.16) | copy-start | bytes 2359300
  18.6 1.8 copy-start
  20.4 0.8 copy-start.13
  20.4 0.8 copy-start.14
  37.0 1.7 copy-start.1
  83.2 1.8 copy-start.15
  83.2 1.8 copy-start.18
  119.2 2.3 copy-start.17
  123.4 1.7 copy-start.16
  126.9 34.5 %copy-start.3 = (bf16[512,192]{1,0:T(8,128)(2,1)S(1)}, bf16[512,192]{1,0:T(8,128)(2,1)}, u32[]{:S(2)}) copy-start(bf16[512,192]{1,0:T(8,128)(2,1)} %get-tuple-element.46) | copy-start | bytes 589828
  172.3 1.4 copy-start.10
  172.3 1.7 copy-start.2
  196.8 1.8 copy-start.11
  196.8 1.8 copy-start.12
  196.8 2.4 copy-start.5
  247.9 2.1 copy-start.7
  249.0 2.3 copy-start.6
  250.1 2.1 copy-start.9
  251.3 1.7 copy-start.8
where the time goes:
time: 255 us; the launch traced here: 254 us
  Pallas kernels  201 us (79%)
  local copies, waits for them, and re-layouts  20.7 us (8%)
  matrix products  19.9 us (8%)
  other arithmetic  10.4 us (4%)
    pallas_call x7, Pallas kernels, call(): pl.pallas_call(kernel, out_shape=outs, in_specs=[VMEM_SPEC] * len(args),...  187 us
    pallas_call x2, Pallas kernels, attention_call(): pl.pallas_call(kernel, out_shape=outs, in_specs=[pl.BlockSpec(memory_spac...  14.2 us
    unnamed x44, local copies, waits for them, and re-layouts  6.53 us

commit v1 on v0

v1 whole, which is shorter than its diff:
```python
import functools
import math

import jax
import jax.numpy as jnp
from jax import lax
from jax.experimental import pallas as pl
from jax.experimental.pallas import tpu as pltpu
from jax.sharding import PartitionSpec as P

HD = 64


EPSILON = 1e-05
NEGATIVE = -1e30
ROOT_HALF = 0.7071067811865476
ROOT_TWO_PI = 2.5066282746310002
MESH = pl.DeviceIdType.MESH
BF16 = jnp.bfloat16
F32 = jnp.float32
VMEM_SPEC = pl.BlockSpec(memory_space=pltpu.VMEM)
DMA = pltpu.SemaphoreType.DMA


def layer_norm(hidden_in, norm_gain, norm_shift):
    centred = hidden_in - jnp.mean(hidden_in, axis=-1, keepdims=True)
    inverse = lax.rsqrt(jnp.mean(centred * centred, axis=-1, keepdims=True) + EPSILON)
    normed = centred * inverse
    return (normed * norm_gain + norm_shift, normed, inverse)


def norm_back(upstream, normed, inverse, norm_gain):
    scaled = upstream * norm_gain
    return inverse * (
        scaled
        - jnp.mean(scaled, axis=-1, keepdims=True)
        - normed * jnp.mean(scaled * normed, axis=-1, keepdims=True)
    )


def gelu_value(pre_act):
    return 0.5 * pre_act * (1.0 + jax.scipy.special.erf(pre_act * ROOT_HALF))


def gelu_slope(pre_act):
    return (
        0.5 * (1.0 + jax.scipy.special.erf(pre_act * ROOT_HALF))
        + pre_act * jnp.exp(-0.5 * pre_act * pre_act) / ROOT_TWO_PI
    )


def peers_of(axis, size):
    me = lax.axis_index(axis)
    found = []
    for step in range(1, size):
        other = lax.rem(me + step, size)
        found.append((other, {axis: other}))
    return found


def grid_peers(sizes):
    count = sizes["dp"] * sizes["ctx"]
    me = lax.axis_index("dp") * sizes["ctx"] + lax.axis_index("ctx")
    found = []
    for step in range(1, count):
        other = lax.rem(me + step, count)
        found.append((other, {"dp": lax.div(other, sizes["ctx"]), "ctx": lax.rem(other, sizes["ctx"])}))
    return me, found


def greet(groups):
    barrier = pltpu.get_barrier_semaphore()
    total = 0
    for group in groups:
        for _, where in group:
            pl.semaphore_signal(barrier, inc=1, device_id=where, device_id_type=MESH)
            total += 1
    pl.semaphore_wait(barrier, total)


def send_all(pairs, peers, send_sem, recv_sem):
    copies = []
    for step, (other, where) in enumerate(peers):
        source, target = pairs(other)
        copies.append(
            pltpu.make_async_remote_copy(
                src_ref=source,
                dst_ref=target,
                send_sem=send_sem.at[step],
                recv_sem=recv_sem.at[step],
                device_id=where,
                device_id_type=MESH,
            )
        )
        copies[-1].start()
    return copies


def wait_all(copies):
    for copy in copies:
        copy.wait()


def slot_sum(slots, count):
    total = slots[0].astype(F32)
    for index in range(1, count):
        total = total + slots[index].astype(F32)
    return total


def sems(count):
    return [DMA((count,)), DMA((count,))]


def call(kernel, outs, scratch, collective_id, args, name, spec=None):
    return pl.pallas_call(
        kernel,
        out_shape=outs,
        in_specs=[VMEM_SPEC] * len(args),
        out_specs=[VMEM_SPEC] * len(outs),
        scratch_shapes=scratch,
        compiler_params=pltpu.CompilerParams(
            collective_id=collective_id, has_side_effects=True, vmem_limit_bytes=56 * 2**20
        ),
        name=name,
    )(*args)


def shaped(shape, dtype):
    return jax.ShapeDtypeStruct(shape, dtype)


def pair_roles(size):
    me = lax.axis_index("dp")
    partner = me + 1 - 2 * lax.rem(me, 2)
    far = [(lax.rem(me + 2 * step, size), lax.rem(me + size - 2 * step, size)) for step in range(1, size // 2)]
    return me, partner, far


def pair_group(size):
    me, partner, far = pair_roles(size)
    return [(partner, {"dp": partner})] + [(to, {"dp": to}) for to, _ in far]


def remote(source, target, send, recv, where):
    return pltpu.make_async_remote_copy(
        src_ref=source, dst_ref=target, send_sem=send, recv_sem=recv, device_id=where, device_id_type=MESH
    )


def pair_sems(size):
    return sems(1) + sems(max(1, size // 2 - 1)) * 2


def gather_start(size, own_ref, place, sem):
    me, partner, far = pair_roles(size)
    near = remote(own_ref, place(me), sem[0].at[0], sem[1].at[0], {"dp": partner})
    wide = [
        remote(own_ref, place(me), sem[2].at[step], sem[3].at[step], {"dp": to})
        for step, (to, _) in enumerate(far)
    ]
    for copy in wide + [near]:
        copy.start()
    return near, wide


def gather_pass(size, copies, place, sem):
    me, partner, far = pair_roles(size)
    passed = []
    for step, (_, origin) in enumerate(far):
        copies[1][step].wait()
        passed.append(
            remote(place(origin), place(origin), sem[4].at[step], sem[5].at[step], {"dp": partner})
        )
        passed[-1].start()
    return [copies[0]] + passed


LAG = 4
CHUNK = 32


def line_roles(size):
    me = lax.axis_index("tensor")
    lower, upper = lax.rem(me + size - 1, size), lax.rem(me + 1, size)
    return [(me, lower, upper), (size - 1 - me, upper, lower)]


def greet_line(size, groups):
    me = lax.axis_index("tensor")
    barrier = pltpu.get_barrier_semaphore()

    @pl.when(me > 0)
    def _():
        pl.semaphore_signal(barrier, inc=1, device_id={"tensor": me - 1}, device_id_type=MESH)

    @pl.when(me < size - 1)
    def _():
        pl.semaphore_signal(barrier, inc=1, device_id={"tensor": me + 1}, device_id_type=MESH)

    total = 0
    for group in groups:
        for _, where in group:
            pl.semaphore_signal(barrier, inc=1, device_id=where, device_id_type=MESH)
            total += 1

    beside = jnp.where(me > 0, 1, 0) + jnp.where(me < size - 1, 1, 0)
    pl.semaphore_wait(barrier, total + beside)


def both(*conditions):
    return functools.reduce(jnp.logical_and, conditions)


def line_start(size, part, slots, sem):
    count = part.shape[1]
    for flow, (place, toward, _) in enumerate(line_roles(size)):

        @pl.when(place == size - 1)
        def _(flow=flow, toward=toward):
            @pl.loop(0, count)
            def _(k):
                remote(
                    part.at[flow, k], slots.at[flow, k], sem[0].at[flow, k], sem[1].at[flow, k], {"tensor": toward}
                ).start()


def line_start_block(size, part, slots, sem, flow, begin, count):
    me = lax.axis_index("tensor")
    lower, upper = lax.rem(me + size - 1, size), lax.rem(me + 1, size)
    place = jnp.where(flow == 0, me, size - 1 - me)
    toward = jnp.where(flow == 0, lower, upper)

    @pl.when(place == size - 1)
    def _():
        @pl.loop(0, count)
        def _(step):
            k = begin + step
            remote(
                part.at[flow, k], slots.at[flow, k], sem[0].at[flow, k], sem[1].at[flow, k], {"tensor": toward}
            ).start()


def line_run(size, part, slots, sums, full, sem, finish, between=(), work=None):
    count = part.shape[1]
    roles = line_roles(size)

    def reduce_copy(flow, k, source):
        return remote(
            source.at[flow, k], slots.at[flow, k], sem[0].at[flow, k], sem[1].at[flow, k], {"tensor": roles[flow][1]}
        )

    def spread_copy(flow, k):
        return remote(
            full.at[flow, k], full.at[flow, k], sem[2].at[flow, k], sem[3].at[flow, k], {"tensor": roles[flow][2]}
        )

    def one_step(step):
        if work is not None:
            work(step)

        for flow, (place, _, _) in enumerate(roles):
            k = step - LAG * (size - 1 - place)
            inside = both(k >= 0, k < count)

            @pl.when(both(inside, place > 0, place < size - 1))
            def _(flow=flow, k=k):
                reduce_copy(flow, k, sums).wait_recv()
                sums[flow, k] = (slots[flow, k].astype(F32) + part[flow, k].astype(F32)).astype(BF16)
                reduce_copy(flow, k, sums).start()

            @pl.when(both(inside, place == 0))
            def _(flow=flow, k=k):
                reduce_copy(flow, k, sums).wait_recv()
                full[flow, k] = finish(flow, k, slots[flow, k].astype(F32) + part[flow, k].astype(F32))
                spread_copy(flow, k).start()

        for flow, (place, _, _) in enumerate(roles):
            k = step - LAG * (size - 1) - LAG * place
            inside = both(k >= 0, k < count, place > 0)

            @pl.when(inside)
            def _(flow=flow, k=k):
                spread_copy(flow, k).wait_recv()

            @pl.when(both(inside, place < size - 1))
            def _(flow=flow, k=k):
                spread_copy(flow, k).start()

    begun, last = 0, count + 2 * LAG * (size - 1)
    for stop, action in tuple(between) + ((last, None),):
        stop = min(stop, last)
        pl.loop(begun, stop)(one_step)
        begun = stop
        if action is not None:
            action()

    for flow, (place, _, _) in enumerate(roles):

        @pl.when(place > 0)
        def _(flow=flow):
            @pl.loop(0, count)
            def _(k):
                reduce_copy(flow, k, sums).wait_send()

        @pl.when(place < size - 1)
        def _(flow=flow):
            @pl.loop(0, count)
            def _(k):
                spread_copy(flow, k).wait_send()


def spread_start(size, mine, full, sem):
    for flow, (place, _, away) in enumerate(line_roles(size)):

        @pl.when(place == 0)
        def _(flow=flow, away=away):
            @pl.loop(0, mine.shape[0])
            def _(k):
                remote(
                    mine.at[k], full.at[flow, k], sem[0].at[flow, k], sem[1].at[flow, k], {"tensor": away}
                ).start()
                full[flow, k] = mine[k]


def spread_run(size, mine, full, sem):
    count = mine.shape[0]
    roles = line_roles(size)

    def pass_on(flow, k):
        return remote(
            full.at[flow, k], full.at[flow, k], sem[0].at[flow, k], sem[1].at[flow, k], {"tensor": roles[flow][2]}
        )

    @pl.loop(0, count + LAG * (size - 1))
    def _(step):
        for flow, (place, _, _) in enumerate(roles):
            k = step - LAG * place
            inside = both(k >= 0, k < count, place > 0)

            @pl.when(inside)
            def _(flow=flow, k=k):
                pass_on(flow, k).wait_recv()

            @pl.when(both(inside, place < size - 1))
            def _(flow=flow, k=k):
                pass_on(flow, k).start()

    for flow, (place, _, _) in enumerate(roles):

        @pl.when(place < size - 1)
        def _(flow=flow):
            @pl.loop(0, count)
            def _(k):
                pass_on(flow, k).wait_send()


def line_sems(count, kinds):
    return [DMA((2, count))] * kinds


def add_row(vector_ref, index, value):
    vector_ref[index : index + 1] += jnp.sum(value, axis=0, keepdims=True)


CONTRACT_LAST = (((1,), (1,)), ((), ()))
CONTRACT_FIRST = (((0,), (0,)), ((), ()))


PIECES = 4
GROUP = 4
ROW_BLOCK = 256


def matmul(left, right):
    return jnp.dot(left, right, preferred_element_type=F32)


def matmul_last(left, right):
    return lax.dot_general(left, right, CONTRACT_LAST, preferred_element_type=F32)


def matmul_first(left, right):
    return lax.dot_general(left, right, CONTRACT_FIRST, preferred_element_type=F32)


def part_rows(index, count):
    return pl.ds(pl.multiple_of(index * count, count), count)


def block_of(step, group):
    return lax.rem(step, 2), lax.div(step, 2) * group


def gather_kernel(sizes, tokens, qkv, proj, wide_tokens, wide_qkv, wide_proj, *sem):
    data, blocks, ranks = sizes["dp"], sizes["ctx"], sizes["tensor"]
    me, rank = lax.axis_index("ctx"), lax.axis_index("tensor")
    mate = rank + 1 - 2 * lax.rem(rank, 2)
    peers = peers_of("ctx", blocks)
    piece = qkv.shape[1]
    rows = tokens.shape[0] // 2 // PIECES

    def span(parity, index):
        return pl.ds(pl.multiple_of((parity * PIECES + index) * rows, rows), rows)

    own_half = lax.rem(rank, 2)
    greet([peers, [(mate, {"tensor": mate})], pair_group(data)])
    across = []
    for index in range(PIECES):
        for step, (_, where) in enumerate(peers):
            here = span(own_half, index)
            across.append(
                remote(tokens.at[here], wide_tokens.at[me, here], sem[0].at[step, index], sem[1].at[step, index], where)
            )
            across[-1].start()
    place_qkv = lambda index: wide_qkv.at[:, part_rows(index, piece)]
    place_proj = lambda index: wide_proj.at[index]
    copies = gather_start(data, qkv, place_qkv, sem[4:10])
    projs = gather_start(data, proj, place_proj, sem[10:16])
    mine = lax.axis_index("dp")
    wide_qkv[:, part_rows(mine, piece)] = qkv[...]
    wide_proj[mine] = proj[...]
    wide_tokens[me] = tokens[...]
    passed = []
    for index in range(PIECES):
        for step in range(len(peers)):
            origin = lax.rem(me + blocks - step - 1, blocks)
            across[index * len(peers) + step].wait_recv()
            here = span(own_half, index)
            place = wide_tokens.at[origin, here]
            passed.append(
                remote(place, place, sem[2].at[step, index], sem[3].at[step, index], {"tensor": mate})
            )
            passed[-1].start()
    passing = gather_pass(data, copies, place_qkv, sem[4:10])
    passing += gather_pass(data, projs, place_proj, sem[10:16])
    for copy in across:
        copy.wait_send()
    wait_all(passed)
    wait_all(passing)


def forward_kernel(
    sizes, score_scale, length_ref, tokens, wide_tokens, wide_qkv, wide_proj, fixed,
    q_ref, k_ref, v_ref, out_ref, low_ref, log_ref, part_ref, proj_ref, flat_ref
):
    length = length_ref[0]
    rows, width = q_ref.shape
    keys = k_ref.shape[0]
    block = math.gcd(rows, ROW_BLOCK)
    column = wide_proj.shape[2]
    for index in range(sizes["dp"]):
        proj_ref[:, index * column : (index + 1) * column] = wide_proj[index]
    for slot, index in enumerate((1, 2, 0)):
        flat_ref[:, slot * width : (slot + 1) * width] = wide_qkv[index]

    @pl.loop(0, keys // block)
    def _(step):
        here = part_rows(step, block)
        found = wide_tokens[here]
        k_ref[here] = matmul(found, wide_qkv[1]).astype(BF16)
        v_ref[here] = (matmul(found, wide_qkv[2]) + fixed[8:9, :width]).astype(BF16)

    hidden_keys = lax.broadcasted_iota(jnp.int32, (block, keys), 1) >= length

    @pl.loop(0, rows // block)
    def _(step):
        here = part_rows(step, block)
        q_ref[here] = (matmul(tokens[here], wide_qkv[0]) + fixed[7:8, :width]).astype(BF16)
        for head in range(width // HD):
            lanes = slice(head * HD, (head + 1) * HD)
            scores = matmul_last(q_ref[here, lanes], k_ref[:, lanes]) * score_scale
            scores = jnp.where(hidden_keys, NEGATIVE, scores)
            top = jnp.max(scores, axis=-1, keepdims=True)
            weights = jnp.exp(scores - top)
            total = jnp.sum(weights, axis=-1, keepdims=True)
            attended = matmul(weights.astype(BF16), v_ref[:, lanes]) / total
            out_ref[here, lanes] = attended
            low_ref[here, lanes] = attended.astype(BF16)
            log_ref[here, head : head + 1] = top + jnp.log(total)
        part_ref[here] = matmul(low_ref[here], proj_ref[...]).astype(BF16)


def near_start(size, grads, chip, sem):
    _, partner, _ = pair_roles(size)
    piece = chip.shape[1]
    copies = [
        remote(
            grads.at[part_rows(2 * index + lax.rem(partner, 2), piece)],
            chip.at[index],
            sem[0].at[index],
            sem[1].at[index],
            {"dp": partner},
        )
        for index in range(size // 2)
    ]
    for copy in copies:
        copy.start()
    return copies


def far_start(size, copies, grads, chip, merged, slots, sem):
    me, _, far = pair_roles(size)
    piece = chip.shape[1]
    wait_all(copies)
    for index in range(size // 2):
        own = grads[part_rows(2 * index + lax.rem(me, 2), piece)]
        merged[index] = (own.astype(F32) + chip[index].astype(F32)).astype(BF16)
    moving = [
        remote(
            merged.at[lax.div(to, 2)], slots.at[lax.div(me, 2)], sem[2].at[step], sem[3].at[step], {"dp": to}
        )
        for step, (to, _) in enumerate(far)
    ]
    for copy in moving:
        copy.start()
    slots[lax.div(me, 2)] = merged[lax.div(me, 2)]
    return moving


def blocks_start(sizes, value, blocks, sem):
    me = lax.axis_index("ctx")
    blocks[me] = value
    return send_all(
        lambda other: (blocks.at[me], blocks.at[me]), peers_of("ctx", sizes["ctx"]), sem[0], sem[1]
    )


def middle_kernel(
    sizes, part, tokens, cotangent, fixed, up, down,
    attn_low, attn_ref, output_ref, vector_ref, block_up, block_down,
    wide_up, wide_down, low, normed_ref, inverse_ref, out_ref, pre, hidden,
    part_two, back_ref, second_low, d_pre, part_three, grads_up, grads_down,
    slots, sums, slots_two, sums_two, slots_three, sums_three,
    chip_a, chip_b, merged_a, merged_b, far_a, far_b, *sem
):
    size, data = sizes["tensor"], sizes["dp"]
    mine = lax.axis_index("dp")
    piece = up.shape[0]
    chunks, chunk, model = part.shape[1:]
    group = math.gcd(chunks, GROUP)
    count = group * chunk
    steps = 2 * chunks // group
    line_one, line_two, line_three = sem[0:4], sem[4:8], sem[8:12]
    sem_up, sem_down = sem[12:18], sem[18:24]
    sem_a, sem_b = sem[24:28], sem[28:32]
    greet_line(size, [pair_group(data)])
    line_start(size, part, slots, line_one)
    place_up = lambda index: wide_up.at[part_rows(index, piece)]
    place_down = lambda index: wide_down.at[part_rows(index, piece)]
    ups = gather_start(data, up, place_up, sem_up)
    downs = gather_start(data, down, place_down, sem_down)
    wide_up[part_rows(mine, piece)] = up[...]
    wide_down[part_rows(mine, piece)] = down[...]
    vector_ref[...] = jnp.zeros_like(vector_ref)

    def first_finish(flow, k, total):
        first_sum = tokens[flow, k].astype(F32) + total + fixed[0:1, :model]
        first_out, normed, inverse = layer_norm(first_sum, fixed[1:2, :model], fixed[2:3, :model])
        out_ref[k] = first_out
        normed_ref[k] = normed
        inverse_ref[k] = inverse
        return first_out.astype(BF16)

    passed = []

    def hand_over():
        passed.extend(gather_pass(data, ups, place_up, sem_up))
        passed.extend(gather_pass(data, downs, place_down, sem_down))

    line_run(size, part, slots, sums, low, line_one, first_finish, [(LAG * size, hand_over)])
    wait_all(passed)

    @pl.loop(0, steps)
    def _(step):
        flow, begin = block_of(step, group)
        here = pl.ds(pl.multiple_of(step * count, count), count)
        found = low[flow, pl.ds(begin, group)].reshape(count, model)
        value = matmul(found, wide_up[...]) + fixed[6:7, : pre.shape[1]]
        pre[here] = value
        hidden[here] = gelu_value(value).astype(BF16)
        result = matmul_last(hidden[here], wide_down[...]).astype(BF16)
        part_two[flow, pl.ds(begin, group)] = result.reshape(group, chunk, model)
        line_start_block(size, part_two, slots_two, line_two, flow, begin, group)

    def second_finish(flow, k, total):
        second_sum = out_ref[k] + total + fixed[3:4, :model]
        result, normed, inverse = layer_norm(second_sum, fixed[4:5, :model], fixed[5:6, :model])
        upstream = cotangent[flow, k].astype(F32)
        d_second = norm_back(upstream, normed, inverse, fixed[4:5, :model])
        output_ref[k] = result.astype(BF16)
        back_ref[k] = d_second
        add_row(vector_ref, 0, upstream)
        add_row(vector_ref, 1, upstream * normed)
        add_row(vector_ref, 2, d_second)
        return d_second.astype(BF16)

    def slope_work(step):
        @pl.when(step < 2 * chunks)
        def _():
            here = part_rows(step, chunk)
            pre[here] = gelu_slope(pre[here])

    line_run(size, part_two, slots_two, sums_two, second_low, line_two, second_finish, work=slope_work)

    @pl.loop(0, steps)
    def _(step):
        flow, begin = block_of(step, group)
        here = pl.ds(pl.multiple_of(step * count, count), count)
        found = second_low[flow, pl.ds(begin, group)].reshape(count, model)
        value = matmul(found, wide_down[...]) * pre[here]
        add_row(vector_ref, 6, value)
        d_pre[here] = value.astype(BF16)
        result = matmul_last(d_pre[here], wide_up[...]).astype(BF16)
        part_three[flow, pl.ds(begin, group)] = result.reshape(group, chunk, model)
        line_start_block(size, part_three, slots_three, line_three, flow, begin, group)

    def third_finish(flow, k, total):
        d_first = total + back_ref[k]
        normed = normed_ref[k]
        d_attn = norm_back(d_first, normed, inverse_ref[k], fixed[1:2, :model])
        attn_ref[k] = d_attn
        add_row(vector_ref, 3, d_first)
        add_row(vector_ref, 4, d_first * normed)
        add_row(vector_ref, 5, d_attn)
        return d_attn.astype(BF16)

    pieces = model // 128

    def grads_work(step):
        @pl.when(step < pieces)
        def _():
            columns = part_rows(step, 128)
            left = [
                second_low[block % 2, block // 2 * group : block // 2 * group + group, :, columns].reshape(count, 128)
                for block in range(steps)
            ]
            grads_down[columns] = matmul_first(jnp.concatenate(left, axis=0), hidden[...]).astype(BF16)

        @pl.when(jnp.logical_and(step >= pieces, step < 2 * pieces))
        def _():
            columns = part_rows(step - pieces, 128)
            left = [
                low[block % 2, block // 2 * group : block // 2 * group + group, :, columns].reshape(count, 128)
                for block in range(steps)
            ]
            grads_up[columns] = matmul_first(jnp.concatenate(left, axis=0), d_pre[...]).astype(BF16)

    near_a, near_b, moving_a, moving_b = [], [], [], []

    def near_down():
        near_b.extend(near_start(data, grads_down, chip_b, sem_b))

    def near_up():
        near_a.extend(near_start(data, grads_up, chip_a, sem_a))
        moving_b.extend(far_start(data, near_b, grads_down, chip_b, merged_b, far_b, sem_b))

    def far_up():
        moving_a.extend(far_start(data, near_a, grads_up, chip_a, merged_a, far_a, sem_a))

    between = [(pieces, near_down), (2 * pieces, near_up), (2 * pieces + LAG, far_up)]
    line_run(
        size, part_three, slots_three, sums_three, attn_low, line_three, third_finish, between, work=grads_work
    )
    wait_all(moving_b)
    block_down[...] = slot_sum(far_b, data // 2).astype(BF16)
    wait_all(moving_a)
    block_up[...] = slot_sum(far_a, data // 2).astype(BF16)


def backward_kernel(
    sizes, score_scale, length_ref, q_ref, k_ref, v_ref, attended_ref, low_ref, log_ref,
    proj_ref, attn_low, tokens, vectors,
    stack_ref, grads_ref, vector_ref,
    dk_ref, dv_ref, heads_ref
):
    length = length_ref[0]
    rows, width = q_ref.shape
    keys = k_ref.shape[0]
    me = lax.axis_index("ctx")
    block = math.gcd(rows, ROW_BLOCK)
    hidden_keys = lax.broadcasted_iota(jnp.int32, (block, keys), 1) >= length
    dk_ref[...] = jnp.zeros_like(dk_ref)
    dv_ref[...] = jnp.zeros_like(dv_ref)
    vector_ref[...] = vectors[...]
    stack_ref[:, 2 * width :] = jnp.zeros((keys, width), BF16)

    @pl.loop(0, rows // block)
    def _(step):
        here = part_rows(step, block)
        there = pl.ds(pl.multiple_of(me * rows + step * block, block), block)
        heads_ref[here] = matmul_last(attn_low[here], proj_ref[...]).astype(BF16)
        for head in range(width // HD):
            lanes = slice(head * HD, (head + 1) * HD)
            q, k, v, d_heads = q_ref[here, lanes], k_ref[:, lanes], v_ref[:, lanes], heads_ref[here, lanes]
            delta = jnp.sum(d_heads.astype(F32) * attended_ref[here, lanes], axis=-1, keepdims=True)
            scores = matmul_last(q, k) * score_scale
            scores = jnp.where(hidden_keys, NEGATIVE, scores)
            probs = jnp.exp(scores - log_ref[here, head : head + 1])
            d_scores = (probs * (matmul_last(d_heads, v) - delta)).astype(BF16)
            dv_ref[:, lanes] += matmul_first(probs.astype(BF16), d_heads)
            dk_ref[:, lanes] += matmul_first(d_scores, q) * score_scale
            d_query = matmul(d_scores, k) * score_scale
            vector_ref[7:8, lanes] += jnp.sum(d_query, axis=0, keepdims=True)
            stack_ref[there, 2 * width + head * HD : 2 * width + (head + 1) * HD] = d_query.astype(BF16)

    vector_ref[7:8, width : 2 * width] = jnp.sum(dv_ref[...], axis=0, keepdims=True)
    stack_ref[:, :width] = dk_ref[...].astype(BF16)
    stack_ref[:, width : 2 * width] = dv_ref[...].astype(BF16)

    @pl.loop(0, grads_ref.shape[0] // 128)
    def _(index):
        columns = part_rows(index, 128)
        grads_ref[columns, : 3 * width] = matmul_first(tokens[:, columns], stack_ref[...]).astype(BF16)
        grads_ref[columns, 3 * width :] = matmul_first(attn_low[:, columns], low_ref[...]).astype(BF16)


def last_kernel(
    sizes, stack, flat, d_attn, grads, block_a, block_b, vectors, mine,
    full, output_ref, owned, owned_a, owned_b, vector_ref,
    part, slots, sums, keys, total_ref, chip, merged, far, blocks, blocks_a, blocks_b, slots_v, grid_v, *sem
):
    size, data = sizes["tensor"], sizes["dp"]
    me, block = lax.axis_index("tensor"), lax.axis_index("ctx")
    chunks, chunk, model = part.shape[1:]
    group = math.gcd(chunks, GROUP)
    count = group * chunk
    steps = 2 * chunks // group
    wide = keys.shape[2]
    line, spread, sem_keys, sem_grads = sem[0:4], sem[4:6], sem[6:8], sem[8:12]
    sem_small, sem_grid, sem_a, sem_b, sem_last = sem[12:14], sem[14:16], sem[16:18], sem[18:20], sem[20:22]
    rows = peers_of("tensor", size)
    others = peers_of("ctx", sizes["ctx"])
    here, everyone = grid_peers(sizes)
    greet([rows, everyone])

    def span(step):
        flow, begin = step % 2, step // 2 * group
        return slice((flow * chunks + begin) * chunk, (flow * chunks + begin) * chunk + count)

    moving_keys = [
        [
            remote(
                stack.at[other, span(step), 0:wide],
                keys.at[block, span(step)],
                sem_keys[0].at[index, step],
                sem_keys[1].at[index, step],
                where,
            )
            for index, (other, where) in enumerate(others)
        ]
        for step in range(steps)
    ]
    for copies in moving_keys:
        for copy in copies:
            copy.start()
    near = near_start(data, grads, chip, sem_grads)
    spread_start(size, mine, output_ref, spread)
    small = send_all(lambda other: (vectors, slots_v.at[me]), rows, sem_small[0], sem_small[1])
    moving_a = blocks_start(sizes, block_a[...], blocks_a, sem_a)
    moving_b = blocks_start(sizes, block_b[...], blocks_b, sem_b)
    slots_v[me] = vectors[...]
    state = {}

    def send_group(step):
        flow, begin = step % 2, step // 2 * group
        there = span(step)
        keys[block, there] = stack[block, there, 0:wide]
        for copy in moving_keys[step]:
            copy.wait_recv()
        total = keys[0, there].astype(F32)
        for index in range(1, sizes["ctx"]):
            total = total + keys[index, there].astype(F32)
        total_ref[there, 0:wide] = total.astype(BF16)
        total_ref[there, wide:] = stack[block, there, wide:]
        result = matmul_last(total_ref[there], flat[...]).astype(BF16)
        part[flow, begin : begin + group] = result.reshape(group, chunk, model)
        line_start_block(size, part, slots, line, flow, begin, group)

    def go_far():
        state["far"] = far_start(data, near, grads, chip, merged, far, sem_grads)
        wait_all(small)
        own = vectors[...]
        row_ids = lax.broadcasted_iota(jnp.int32, own.shape, 0)
        grid_v[here] = jnp.where(row_ids < 6, slot_sum(slots_v, size), own)
        state["small"] = send_all(
            lambda other: (grid_v.at[here], grid_v.at[here]), everyone, sem_grid[0], sem_grid[1]
        )

    def go_across():
        wait_all(state["far"])
        value = slot_sum(far, data // 2).astype(BF16)
        state["across"] = blocks_start(sizes, value, blocks, sem_last)

    def finish(flow, k, total):
        return (total + d_attn[k]).astype(BF16)

    for step in range(2):
        send_group(step)
    between = [(1, go_far)]
    between += [(LAG + 2 * step - 3, functools.partial(send_group, step)) for step in range(2, steps)]
    between += [(max(LAG * size, LAG + 2 * steps), go_across)]
    line_run(size, part, slots, sums, full, line, finish, between)
    spread_run(size, mine, output_ref, spread)
    for copies in moving_keys:
        for copy in copies:
            copy.wait_send()
    wait_all(state["small"])
    vector_ref[...] = slot_sum(grid_v, data * sizes["ctx"])
    wait_all(moving_a)
    owned_a[...] = slot_sum(blocks_a, sizes["ctx"])
    wait_all(moving_b)
    owned_b[...] = slot_sum(blocks_b, sizes["ctx"])
    wait_all(state["across"])
    owned[...] = slot_sum(blocks, sizes["ctx"])


def unpack_kernel(
    full, output, owned, owned_a, owned_b,
    output_ref, tokens_ref, qkv_ref, proj_ref, up_ref, down_ref
):
    width = qkv_ref.shape[2]
    output_ref[...] = output[...]
    tokens_ref[...] = full[...].astype(F32)
    for index, slot in enumerate((2, 0, 1)):
        qkv_ref[index] = owned[:, slot * width : (slot + 1) * width]
    proj_ref[...] = owned[:, 3 * width :].T
    up_ref[...] = owned_a[...]
    down_ref[...] = owned_b[...]


def local_call(kernel, outs, scratch, args, name, scalars=1):
    return pl.pallas_call(
        kernel,
        out_shape=outs,
        in_specs=[pl.BlockSpec(memory_space=pltpu.SMEM)] * scalars + [VMEM_SPEC] * (len(args) - scalars),
        out_specs=[VMEM_SPEC] * len(outs),
        scratch_shapes=scratch,
        compiler_params=pltpu.CompilerParams(vmem_limit_bytes=60 * 2**20),
        name=name,
    )(*args)


def per_device(
    sizes,
    tokens,
    lengths,
    cotangent,
    qkv_weight,
    query_bias,
    value_bias,
    proj_weight,
    proj_bias,
    first_gain,
    first_shift,
    up_weight,
    up_bias,
    down_weight,
    down_bias,
    second_gain,
    second_shift,
):
    data, blocks, ranks = sizes["dp"], sizes["ctx"], sizes["tensor"]
    rows_in = tokens[0]
    row_count, model = rows_in.shape
    half = row_count // 2
    chunk = math.gcd(half, CHUNK)
    chunks = half // chunk
    piece, width = qkv_weight.shape[1:]
    up_width = up_weight.shape[1]
    keys = blocks * row_count
    score_scale = 1.0 / math.sqrt(HD)
    split = (2, chunks, chunk, model)
    flow = pltpu.VMEM(split, BF16)
    line = line_sems(chunks, 4)
    local = shaped(split[1:], F32)
    held = pltpu.VMEM(split[1:], F32)
    steps = 2 * chunks // math.gcd(chunks, GROUP)
    vector_width = max(model, up_width, 2 * width)
    fixed = jnp.zeros((16, vector_width), F32)
    row_ids = lax.broadcasted_iota(jnp.int32, fixed.shape, 0)
    for index, vector in enumerate(
        [
            proj_bias, first_gain, first_shift, down_bias, second_gain, second_shift,
            up_bias, query_bias, value_bias,
        ]
    ):
        padded = jnp.pad(vector, (0, vector_width - vector.shape[0]))
        fixed = jnp.where(row_ids == index, padded[None], fixed)

    wide_tokens, wide_qkv, wide_proj = call(
        functools.partial(gather_kernel, sizes),
        [
            shaped((blocks, row_count, model), BF16),
            shaped((3, model, width), BF16),
            shaped((data,) + proj_weight.shape, BF16),
        ],
        [DMA((blocks - 1, PIECES))] * 4 + pair_sems(data) * 2,
        0,
        (rows_in, qkv_weight, proj_weight),
        "gather_inputs",
    )
    wide_tokens = wide_tokens.reshape(keys, model)
    queries, key_rows, value_rows, attended, attended_low, log_total, attn_part, flat_proj, flat_qkv = local_call(
        functools.partial(forward_kernel, sizes, score_scale),
        [
            shaped((row_count, width), BF16),
            shaped((keys, width), BF16),
            shaped((keys, width), BF16),
            shaped((row_count, width), F32),
            shaped((row_count, width), BF16),
            shaped((row_count, width // HD), F32),
            shaped((row_count, model), BF16),
            shaped((width, model), BF16),
            shaped((model, 3 * width), BF16),
        ],
        [],
        (lengths, rows_in, wide_tokens, wide_qkv, wide_proj, fixed),
        "attention_forward",
    )

    up_shape = (model, up_width)
    pair_slots = pltpu.VMEM((data // 2, model // data, up_width), BF16)
    pair_moves = sems(data // 2) + sems(max(1, data // 2 - 1))
    attn_low, d_attn, output_part, vectors, block_up, block_down = call(
        functools.partial(middle_kernel, sizes),
        [
            shaped(split, BF16),
            local,
            shaped(split[1:], BF16),
            shaped((8, vector_width), F32),
            shaped((model // data, up_width), BF16),
            shaped((model // data, up_width), BF16),
        ],
        [
            pltpu.VMEM(up_shape, BF16),
            pltpu.VMEM(up_shape, BF16),
            flow,
            held,
            pltpu.VMEM((chunks, chunk, 1), F32),
            held,
            pltpu.VMEM((row_count, up_width), F32),
            pltpu.VMEM((row_count, up_width), BF16),
            flow,
            held,
            flow,
            pltpu.VMEM((row_count, up_width), BF16),
            flow,
            pltpu.VMEM(up_shape, BF16),
            pltpu.VMEM(up_shape, BF16),
        ]
        + [flow] * 6
        + [pair_slots] * 6
        + line * 3
        + pair_sems(data) * 2
        + pair_moves * 2,
        1,
        (
            attn_part.reshape(split),
            rows_in.reshape(split),
            cotangent[0].reshape(split),
            fixed,
            up_weight,
            down_weight.T,
        ),
        "norms_and_hidden",
    )

    stack, last_grads, vectors = local_call(
        functools.partial(backward_kernel, sizes, score_scale),
        [
            shaped((keys, 3 * width), BF16),
            shaped((model, 4 * width), BF16),
            shaped(vectors.shape, F32),
        ],
        [
            pltpu.VMEM((keys, width), F32),
            pltpu.VMEM((keys, width), F32),
            pltpu.VMEM((row_count, width), BF16),
        ],
        (
            lengths, queries, key_rows, value_rows, attended, attended_low, log_total,
            flat_proj, attn_low.reshape(row_count, model), wide_tokens, vectors,
        ),
        "attention_backward",
    )

    own_shape = (model // data, 4 * width)
    last_pair = pltpu.VMEM((data // 2,) + own_shape, BF16)
    grad_tokens, output, own_last, own_up, own_down, sums = call(
        functools.partial(last_kernel, sizes),
        [
            shaped(split, BF16),
            shaped(split, BF16),
            shaped(own_shape, F32),
            shaped((model // data, up_width), F32),
            shaped((model // data, up_width), F32),
            shaped(vectors.shape, F32),
        ],
        [flow] * 3
        + [
            pltpu.VMEM((blocks, row_count, 2 * width), BF16),
            pltpu.VMEM((row_count, 3 * width), BF16),
        ]
        + [last_pair] * 3
        + [pltpu.VMEM((blocks,) + own_shape, BF16)]
        + [pltpu.VMEM((blocks, model // data, up_width), BF16)] * 2
        + [
            pltpu.VMEM((ranks,) + vectors.shape, F32),
            pltpu.VMEM((data * blocks,) + vectors.shape, F32),
        ]
        + line
        + line_sems(chunks, 2)
        + [DMA((max(1, blocks - 1), steps))] * 2
        + pair_moves
        + sems(ranks - 1)
        + sems(data * blocks - 1)
        + sems(blocks - 1) * 3,
        2,
        (
            stack.reshape(blocks, row_count, 3 * width),
            flat_qkv,
            d_attn,
            last_grads,
            block_up,
            block_down,
            vectors,
            output_part,
        ),
        "token_grads",
    )
    output, grad_tokens, own_qkv, own_proj, own_up, own_down = local_call(
        unpack_kernel,
        [
            shaped((row_count, model), BF16),
            shaped((row_count, model), F32),
            shaped((3, model // data, width), F32),
            shaped((width, model // data), F32),
            shaped(own_up.shape, F32),
            shaped(own_down.shape, F32),
        ],
        [],
        (
            grad_tokens.reshape(row_count, model),
            output.reshape(row_count, model),
            own_last,
            own_up,
            own_down,
        ),
        "unpack",
        scalars=0,
    )
    return (
        output[None],
        grad_tokens[None],
        own_qkv,
        sums[7, :width],
        sums[7, width : 2 * width],
        own_proj,
        sums[5, :model],
        sums[4, :model],
        sums[3, :model],
        own_up,
        sums[6, :up_width],
        own_down.T,
        sums[2, :model],
        sums[1, :model],
        sums[0, :model],
    )


def solution(mesh):
    placed = (
        P("dp", "ctx", None),
        P("dp"),
        P("dp", "ctx", None),
        P(None, "dp", "tensor"),
        P("tensor"),
        P("tensor"),
        P("tensor", "dp"),
        P(),
        P(),
        P(),
        P("dp", "tensor"),
        P("tensor"),
        P("tensor", "dp"),
        P(),
        P(),
        P(),
    )
    return jax.shard_map(
        functools.partial(per_device, dict(mesh.shape)),
        mesh=mesh,
        in_specs=placed,
        out_specs=(
            P("dp", "ctx", None),
            P("dp", "ctx", None),
            P(None, "dp", "tensor"),
            P("tensor"),
            P("tensor"),
            P("tensor", "dp"),
            P(),
            P(),
            P(),
            P("dp", "tensor"),
            P("tensor"),
            P("tensor", "dp"),
            P(),
            P(),
            P(),
        ),
        check_vma=False,
    )
```

time: 255 us -> 201 us (0.79)
  matrix products: 19.9 us -> 0 us
  local copies, waits for them, and re-layouts: 20.7 us -> 4.45 us
  other arithmetic: 10.4 us -> 1.52 us
  Pallas kernels: 201 us -> 193 us
    pallas_call x7 -> x3, Pallas kernels: 187 us -> 167 us  [call(): pl.pallas_call(kernel, out_shape=outs, in_specs=[VMEM_SPEC] * len(args),...]
    dot_general x12 -> x0, matrix products: 19.9 us -> none  [the longest x1 2.26 us: per_device(): jnp.einsum('td,fd->tf', d_second_low, wide_down, preferred_element_type=F32)]
    pallas_call x2 -> x3, Pallas kernels: 14.2 us -> 26.6 us  [local_call(): pl.pallas_call(kernel, out_shape=outs, in_specs=[pl.BlockSpec(memory_spac...]
    unnamed x44 -> x0, local copies, waits for them, and re-layouts: 6.53 us -> none
    convert_element_type x5 -> x0, other arithmetic: 4.66 us -> none  [the longest x1 1.4 us: per_device(): key_grads.astype(BF16)]
    transpose x3 -> x0, local copies, waits for them, and re-layouts: 4.18 us -> none  [the longest x1 1.77 us: per_device(): wide_down = wide_down.transpose(1, 0, 2).reshape(up_width, model)]
    concatenate x5 -> x0, other arithmetic: 2.87 us -> none  [the longest x1 1.19 us: per_device(): jnp.concatenate([key_grads.astype(BF16), value_grads.astype(BF16)], axis=1)]
where the time goes in v1:
time: 201 us
  Pallas kernels  193 us (96%)
  local copies, waits for them, and re-layouts  4.45 us (2%)
    pallas_call x3, Pallas kernels, call(): pl.pallas_call(kernel, out_shape=outs, in_specs=[VMEM_SPEC] * len(args),...  167 us
    pallas_call x3, Pallas kernels, local_call(): pl.pallas_call(kernel, out_shape=outs, in_specs=[pl.BlockSpec(memory_spac...  26.6 us

profile of v1, /device:TPU:0, one launch (start us, length us, event | category | flops | bytes accessed | tf_op | source)
XLA Modules:
  0.0 200.6 jit_solution(9334881718580556855)
XLA Ops:
  1.4 0.7 pad.8
  2.0 0.7 pad.7
  2.7 1.5 select_select_fusion.fixed
  4.2 21.1 %gather_inputs.1 = (bf16[2,512,768]{2,1,0:T(8,128)(2,1)}, bf16[3,768,192]{2,1,0:T(8,128)(2,1)}, bf16[4,192,192]{2,1,0:T(8,128)(2,1)}) custom-call(bf16[512,768]{1,0:T(8,128)(2,1)} %bitcast.15, bf16[3,192,192]{2,1,0:T(8,128)(2,1)} %qkv.1, bf16[192,192]{1,0:T(8,128)(2,1)} %proj.1), custom_call_target="tpu_custom_call" | custom-call | tf_op jit(solution)/shard_map/gather_inputs/pallas_call | solution.py:116
  25.3 10.0 %attention_forward.1 = (bf16[512,192]{1,0:T(8,128)(2,1)}, bf16[1024,192]{1,0:T(8,128)(2,1)}, bf16[1024,192]{1,0:T(8,128)(2,1)}, f32[512,192]{1,0:T(8,128)}, bf16...) custom-call(s32[1]{0:T(128)S(6)} %copy.31.length_ref, ...), custom_call_target="tpu_custom_call" | custom-call | tf_op jit(solution)/shard_map/attention_forward/pallas_call | solution.py:833
  35.3 89.6 %norms_and_hidden.1 = (bf16[2,8,32,768]{3,2,1,0:T(8,128)(2,1)}, f32[8,32,768]{2,1,0:T(8,128)}, bf16[8,32,768]{2,1,0:T(8,128)(2,1)}, f32[8,768]{1,0:T(8,128)}, bf...) custom-call(bf16[2,8,32,768]{3,2,1,0:T(8,128)(2,1)} %bitcast.24, bf16[2,8,32,768]{3,2,1,0:T(8,128)(2,1)} %bitcast.17, ...), custom_call_target="tpu_custom_call" | custom-call | tf_op jit(solution)/shard_map/norms_and_hidden/pallas_call | solution.py:116
  124.9 12.4 %attention_backward.1 = (bf16[1024,576]{1,0:T(8,128)(2,1)}, bf16[768,768]{1,0:T(8,128)(2,1)}, f32[8,768]{1,0:T(8,128)}) custom-call(s32[1]{0:T(128)S(6)} %copy.31.length_ref, bf16[512,192]{1,0:T(8,128)(2,1)} %get-tuple-element.51.q_ref, bf16[1024,192]{1,0:T(8,128)(2,1)} %get-tuple-element.52.k_ref, bf16[1024,192]{1,0:T(8,128)(2,1)} %get-tuple-element.53.v_ref, ...), custom_call_target="tpu_custom_call" | custom-call | tf_op jit(solution)/shard_map/attention_backward/pallas_call | solution.py:833
  137.3 56.0 %token_grads.1 = (bf16[2,8,32,768]{3,2,1,0:T(8,128)(2,1)}, bf16[2,8,32,768]{3,2,1,0:T(8,128)(2,1)}, f32[192,768]{1,0:T(8,128)}, f32[192,768]{1,0:T(8,128)}, f32[192,768]{1,0:T(8,128)}, /*index=5*/f32[8,768]{1,0:T(8,128)}) custom-call(bf16[2,512,576]{2,1,0:T(8,128)(2,1)} %bitcast.20, bf16[768,576]{1,0:T(8,128)(2,1)} %get-tuple-element.62.flat, ...), custom_call_target="tpu_custom_call" | custom-call | tf_op jit(solution)/shard_map/token_grads/pallas_call | solution.py:116
  193.3 1.4 fusion
  194.7 1.7 slice_reduce_fusion
  196.4 4.2 %unpack.1 = (bf16[512,768]{1,0:T(8,128)(2,1)}, f32[512,768]{1,0:T(8,128)}, f32[3,192,192]{2,1,0:T(8,128)}, f32[192,192]{1,0:T(8,128)}, f32[192,768]{1,0:T(8,128)}, /*index=5*/f32[192,768]{1,0:T(8,128)}) custom-call(bf16[512,768]{1,0:T(8,128)(2,1)} %bitcast.22, bf16[512,768]{1,0:T(8,128)(2,1)} %bitcast.23, f32[192,768]{1,0:T(8,128)} %get-tuple-element.71.owned, ...), custom_call_target="tpu_custom_call" | custom-call | tf_op jit(solution)/shard_map/unpack/pallas_call | solution.py:833
  (5 shorter events, 0.0 us)

commit v2 on v1

--- a/solution.py
+++ b/solution.py
@@ -112,15 +112,15 @@
     return [DMA((count,)), DMA((count,))]
 
 
-def call(kernel, outs, scratch, collective_id, args, name, spec=None):
+def call(kernel, outs, scratch, collective_id, args, name, scalars=0):
     return pl.pallas_call(
         kernel,
         out_shape=outs,
-        in_specs=[VMEM_SPEC] * len(args),
+        in_specs=[pl.BlockSpec(memory_space=pltpu.SMEM)] * scalars + [VMEM_SPEC] * (len(args) - scalars),
         out_specs=[VMEM_SPEC] * len(outs),
         scratch_shapes=scratch,
         compiler_params=pltpu.CompilerParams(
-            collective_id=collective_id, has_side_effects=True, vmem_limit_bytes=56 * 2**20
+            collective_id=collective_id, has_side_effects=True, vmem_limit_bytes=62 * 2**20
         ),
         name=name,
     )(*args)
@@ -323,36 +323,37 @@
                 full[flow, k] = mine[k]
 
 
-def spread_run(size, mine, full, sem):
+def spread_copy(size, flow, k, full, sem):
+    toward = line_roles(size)[flow][2]
+    return remote(full.at[flow, k], full.at[flow, k], sem[0].at[flow, k], sem[1].at[flow, k], {"tensor": toward})
+
+
+def spread_steps(size, mine, full, sem, begin, end):
     count = mine.shape[0]
-    roles = line_roles(size)
-
-    def pass_on(flow, k):
-        return remote(
-            full.at[flow, k], full.at[flow, k], sem[0].at[flow, k], sem[1].at[flow, k], {"tensor": roles[flow][2]}
-        )
-
-    @pl.loop(0, count + LAG * (size - 1))
+
+    @pl.loop(begin, end)
     def _(step):
-        for flow, (place, _, _) in enumerate(roles):
-            k = step - LAG * place
+        for flow, (place, _, _) in enumerate(line_roles(size)):
+            k = step - SPREAD_LAG * place
             inside = both(k >= 0, k < count, place > 0)
 
             @pl.when(inside)
             def _(flow=flow, k=k):
-                pass_on(flow, k).wait_recv()
+                spread_copy(size, flow, k, full, sem).wait_recv()
 
             @pl.when(both(inside, place < size - 1))
             def _(flow=flow, k=k):
-                pass_on(flow, k).start()
-
-    for flow, (place, _, _) in enumerate(roles):
+                spread_copy(size, flow, k, full, sem).start()
+
+
+def spread_end(size, mine, full, sem):
+    for flow, (place, _, _) in enumerate(line_roles(size)):
 
         @pl.when(place < size - 1)
         def _(flow=flow):
-            @pl.loop(0, count)
+            @pl.loop(0, mine.shape[0])
             def _(k):
-                pass_on(flow, k).wait_send()
+                spread_copy(size, flow, k, full, sem).wait_send()
 
 
 def line_sems(count, kinds):
@@ -370,6 +371,7 @@
 PIECES = 4
 GROUP = 4
 ROW_BLOCK = 256
+SPREAD_LAG = 2
 
 
 def matmul(left, right):
@@ -441,10 +443,12 @@
 
 
 def forward_kernel(
-    sizes, score_scale, length_ref, tokens, wide_tokens, wide_qkv, wide_proj, fixed,
-    q_ref, k_ref, v_ref, out_ref, low_ref, log_ref, part_ref, proj_ref, flat_ref
+    sizes, score_scale, length_ref, tokens, wide_tokens, wide_qkv, wide_proj, *refs
 ):
+    given, (q_ref, k_ref, v_ref, out_ref, low_ref, log_ref, part_ref, proj_ref, flat_ref, fixed) = refs[:-10], refs[-10:]
     length = length_ref[0]
+    for index, vector in enumerate(given):
+        fixed[index : index + 1, : vector.shape[0]] = vector[...].reshape(1, -1)
     rows, width = q_ref.shape
     keys = k_ref.shape[0]
     block = math.gcd(rows, ROW_BLOCK)
@@ -668,29 +672,48 @@
     block_up[...] = slot_sum(far_a, data // 2).astype(BF16)
 
 
-def backward_kernel(
+def back_kernel(
     sizes, score_scale, length_ref, q_ref, k_ref, v_ref, attended_ref, low_ref, log_ref,
-    proj_ref, attn_low, tokens, vectors,
-    stack_ref, grads_ref, vector_ref,
-    dk_ref, dv_ref, heads_ref
+    proj_ref, attn_low, tokens, vectors, flat, d_attn, block_a, block_b, mine,
+    full, output_ref, owned, owned_a, owned_b, vector_ref,
+    dk_ref, dv_ref, heads_ref, stack, grads, own_ref,
+    part, slots, sums, keys, total_ref, chip, merged, far, blocks, blocks_a, blocks_b, slots_v, grid_v, *sem
 ):
+    size, data = sizes["tensor"], sizes["dp"]
+    rank, me = lax.axis_index("tensor"), lax.axis_index("ctx")
+    chunks, chunk, model = part.shape[1:]
+    group = math.gcd(chunks, GROUP)
+    count = group * chunk
+    steps = 2 * chunks // group
+    wide = keys.shape[2]
+    line, spread, sem_keys, sem_grads = sem[0:4], sem[4:6], sem[6:8], sem[8:12]
+    sem_small, sem_grid, sem_a, sem_b, sem_last = sem[12:14], sem[14:16], sem[16:18], sem[18:20], sem[20:22]
+    others = peers_of("ctx", sizes["ctx"])
+    here_v, everyone = grid_peers(sizes)
+    peers = peers_of("tensor", size)
+    greet([peers, everyone])
+    spread_start(size, mine, output_ref, spread)
+    moving_a = blocks_start(sizes, block_a[...], blocks_a, sem_a)
+    moving_b = blocks_start(sizes, block_b[...], blocks_b, sem_b)
+
     length = length_ref[0]
     rows, width = q_ref.shape
-    keys = k_ref.shape[0]
-    me = lax.axis_index("ctx")
+    total_keys = k_ref.shape[0]
     block = math.gcd(rows, ROW_BLOCK)
-    hidden_keys = lax.broadcasted_iota(jnp.int32, (block, keys), 1) >= length
+    hidden_keys = lax.broadcasted_iota(jnp.int32, (block, total_keys), 1) >= length
     dk_ref[...] = jnp.zeros_like(dk_ref)
     dv_ref[...] = jnp.zeros_like(dv_ref)
-    vector_ref[...] = vectors[...]
-    stack_ref[:, 2 * width :] = jnp.zeros((keys, width), BF16)
+    own_ref[...] = vectors[...]
+    stack[:, :, 2 * width :] = jnp.zeros((sizes["ctx"], rows, width), BF16)
+    heads = width // HD
+    turns = rows // block * heads
+    relays = mine.shape[0] + SPREAD_LAG * (size - 1)
 
     @pl.loop(0, rows // block)
     def _(step):
         here = part_rows(step, block)
-        there = pl.ds(pl.multiple_of(me * rows + step * block, block), block)
         heads_ref[here] = matmul_last(attn_low[here], proj_ref[...]).astype(BF16)
-        for head in range(width // HD):
+        for head in range(heads):
             lanes = slice(head * HD, (head + 1) * HD)
             q, k, v, d_heads = q_ref[here, lanes], k_ref[:, lanes], v_ref[:, lanes], heads_ref[here, lanes]
             delta = jnp.sum(d_heads.astype(F32) * attended_ref[here, lanes], axis=-1, keepdims=True)
@@ -701,38 +724,14 @@
             dv_ref[:, lanes] += matmul_first(probs.astype(BF16), d_heads)
             dk_ref[:, lanes] += matmul_first(d_scores, q) * score_scale
             d_query = matmul(d_scores, k) * score_scale
-            vector_ref[7:8, lanes] += jnp.sum(d_query, axis=0, keepdims=True)
-            stack_ref[there, 2 * width + head * HD : 2 * width + (head + 1) * HD] = d_query.astype(BF16)
-
-    vector_ref[7:8, width : 2 * width] = jnp.sum(dv_ref[...], axis=0, keepdims=True)
-    stack_ref[:, :width] = dk_ref[...].astype(BF16)
-    stack_ref[:, width : 2 * width] = dv_ref[...].astype(BF16)
-
-    @pl.loop(0, grads_ref.shape[0] // 128)
-    def _(index):
-        columns = part_rows(index, 128)
-        grads_ref[columns, : 3 * width] = matmul_first(tokens[:, columns], stack_ref[...]).astype(BF16)
-        grads_ref[columns, 3 * width :] = matmul_first(attn_low[:, columns], low_ref[...]).astype(BF16)
-
-
-def last_kernel(
-    sizes, stack, flat, d_attn, grads, block_a, block_b, vectors, mine,
-    full, output_ref, owned, owned_a, owned_b, vector_ref,
-    part, slots, sums, keys, total_ref, chip, merged, far, blocks, blocks_a, blocks_b, slots_v, grid_v, *sem
-):
-    size, data = sizes["tensor"], sizes["dp"]
-    me, block = lax.axis_index("tensor"), lax.axis_index("ctx")
-    chunks, chunk, model = part.shape[1:]
-    group = math.gcd(chunks, GROUP)
-    count = group * chunk
-    steps = 2 * chunks // group
-    wide = keys.shape[2]
-    line, spread, sem_keys, sem_grads = sem[0:4], sem[4:6], sem[6:8], sem[8:12]
-    sem_small, sem_grid, sem_a, sem_b, sem_last = sem[12:14], sem[14:16], sem[16:18], sem[18:20], sem[20:22]
-    rows = peers_of("tensor", size)
-    others = peers_of("ctx", sizes["ctx"])
-    here, everyone = grid_peers(sizes)
-    greet([rows, everyone])
+            own_ref[7:8, lanes] += jnp.sum(d_query, axis=0, keepdims=True)
+            stack[me, here, 2 * width + head * HD : 2 * width + (head + 1) * HD] = d_query.astype(BF16)
+            turn = step * heads + head
+            spread_steps(size, mine, output_ref, spread, turn * relays // turns, (turn + 1) * relays // turns)
+
+    own_ref[7:8, width : 2 * width] = jnp.sum(dv_ref[...], axis=0, keepdims=True)
+    stack[:, :, :width] = dk_ref[...].astype(BF16).reshape(sizes["ctx"], rows, width)
+    stack[:, :, width : 2 * width] = dv_ref[...].astype(BF16).reshape(sizes["ctx"], rows, width)
 
     def span(step):
         flow, begin = step % 2, step // 2 * group
@@ -742,7 +741,7 @@
         [
             remote(
                 stack.at[other, span(step), 0:wide],
-                keys.at[block, span(step)],
+                keys.at[me, span(step)],
                 sem_keys[0].at[index, step],
                 sem_keys[1].at[index, step],
                 where,
@@ -754,25 +753,30 @@
     for copies in moving_keys:
         for copy in copies:
             copy.start()
+    small = send_all(lambda other: (own_ref, slots_v.at[rank]), peers, sem_small[0], sem_small[1])
+    slots_v[rank] = own_ref[...]
+
+    @pl.loop(0, model // 128)
+    def _(index):
+        columns = part_rows(index, 128)
+        every = stack[...].reshape(total_keys, 3 * width)
+        grads[columns, : 3 * width] = matmul_first(tokens[:, columns], every).astype(BF16)
+        grads[columns, 3 * width :] = matmul_first(attn_low[:, columns], low_ref[...]).astype(BF16)
+
     near = near_start(data, grads, chip, sem_grads)
-    spread_start(size, mine, output_ref, spread)
-    small = send_all(lambda other: (vectors, slots_v.at[me]), rows, sem_small[0], sem_small[1])
-    moving_a = blocks_start(sizes, block_a[...], blocks_a, sem_a)
-    moving_b = blocks_start(sizes, block_b[...], blocks_b, sem_b)
-    slots_v[me] = vectors[...]
     state = {}
 
     def send_group(step):
         flow, begin = step % 2, step // 2 * group
         there = span(step)
-        keys[block, there] = stack[block, there, 0:wide]
+        keys[me, there] = stack[me, there, 0:wide]
         for copy in moving_keys[step]:
             copy.wait_recv()
         total = keys[0, there].astype(F32)
         for index in range(1, sizes["ctx"]):
             total = total + keys[index, there].astype(F32)
         total_ref[there, 0:wide] = total.astype(BF16)
-        total_ref[there, wide:] = stack[block, there, wide:]
+        total_ref[there, wide:] = stack[me, there, wide:]
         result = matmul_last(total_ref[there], flat[...]).astype(BF16)
         part[flow, begin : begin + group] = result.reshape(group, chunk, model)
         line_start_block(size, part, slots, line, flow, begin, group)
@@ -780,11 +784,11 @@
     def go_far():
         state["far"] = far_start(data, near, grads, chip, merged, far, sem_grads)
         wait_all(small)
-        own = vectors[...]
+        own = own_ref[...]
         row_ids = lax.broadcasted_iota(jnp.int32, own.shape, 0)
-        grid_v[here] = jnp.where(row_ids < 6, slot_sum(slots_v, size), own)
+        grid_v[here_v] = jnp.where(row_ids < 6, slot_sum(slots_v, size), own)
         state["small"] = send_all(
-            lambda other: (grid_v.at[here], grid_v.at[here]), everyone, sem_grid[0], sem_grid[1]
+            lambda other: (grid_v.at[here_v], grid_v.at[here_v]), everyone, sem_grid[0], sem_grid[1]
         )
 
     def go_across():
@@ -801,7 +805,7 @@
     between += [(LAG + 2 * step - 3, functools.partial(send_group, step)) for step in range(2, steps)]
     between += [(max(LAG * size, LAG + 2 * steps), go_across)]
     line_run(size, part, slots, sums, full, line, finish, between)
-    spread_run(size, mine, output_ref, spread)
+    spread_end(size, mine, output_ref, spread)
     for copies in moving_keys:
         for copy in copies:
             copy.wait_send()
@@ -816,8 +820,8 @@
 
 
 def unpack_kernel(
-    full, output, owned, owned_a, owned_b,
-    output_ref, tokens_ref, qkv_ref, proj_ref, up_ref, down_ref
+    full, output, owned, owned_a, owned_b, sums,
+    output_ref, tokens_ref, qkv_ref, proj_ref, up_ref, down_ref, query_ref, value_ref, *rows
 ):
     width = qkv_ref.shape[2]
     output_ref[...] = output[...]
@@ -827,6 +831,10 @@
     proj_ref[...] = owned[:, 3 * width :].T
     up_ref[...] = owned_a[...]
     down_ref[...] = owned_b[...]
+    query_ref[...] = sums[7, :width]
+    value_ref[...] = sums[7, width : 2 * width]
+    for index, row in enumerate(rows):
+        row[...] = sums[index, : row.shape[0]]
 
 
 def local_call(kernel, outs, scratch, args, name, scalars=1):
@@ -877,16 +885,9 @@
     held = pltpu.VMEM(split[1:], F32)
     steps = 2 * chunks // math.gcd(chunks, GROUP)
     vector_width = max(model, up_width, 2 * width)
-    fixed = jnp.zeros((16, vector_width), F32)
-    row_ids = lax.broadcasted_iota(jnp.int32, fixed.shape, 0)
-    for index, vector in enumerate(
-        [
-            proj_bias, first_gain, first_shift, down_bias, second_gain, second_shift,
-            up_bias, query_bias, value_bias,
-        ]
-    ):
-        padded = jnp.pad(vector, (0, vector_width - vector.shape[0]))
-        fixed = jnp.where(row_ids == index, padded[None], fixed)
+    given = (
+        proj_bias, first_gain, first_shift, down_bias, second_gain, second_shift, up_bias, query_bias, value_bias
+    )
 
     wide_tokens, wide_qkv, wide_proj = call(
         functools.partial(gather_kernel, sizes),
@@ -901,7 +902,7 @@
         "gather_inputs",
     )
     wide_tokens = wide_tokens.reshape(keys, model)
-    queries, key_rows, value_rows, attended, attended_low, log_total, attn_part, flat_proj, flat_qkv = local_call(
+    queries, key_rows, value_rows, attended, attended_low, log_total, attn_part, flat_proj, flat_qkv, fixed = local_call(
         functools.partial(forward_kernel, sizes, score_scale),
         [
             shaped((row_count, width), BF16),
@@ -913,9 +914,10 @@
             shaped((row_count, model), BF16),
             shaped((width, model), BF16),
             shaped((model, 3 * width), BF16),
+            shaped((16, vector_width), F32),
         ],
         [],
-        (lengths, rows_in, wide_tokens, wide_qkv, wide_proj, fixed),
+        (lengths, rows_in, wide_tokens, wide_qkv, wide_proj) + given,
         "attention_forward",
     )
 
@@ -966,29 +968,10 @@
         "norms_and_hidden",
     )
 
-    stack, last_grads, vectors = local_call(
-        functools.partial(backward_kernel, sizes, score_scale),
-        [
-            shaped((keys, 3 * width), BF16),
-            shaped((model, 4 * width), BF16),
-            shaped(vectors.shape, F32),
-        ],
-        [
-            pltpu.VMEM((keys, width), F32),
-            pltpu.VMEM((keys, width), F32),
-            pltpu.VMEM((row_count, width), BF16),
-        ],
-        (
-            lengths, queries, key_rows, value_rows, attended, attended_low, log_total,
-            flat_proj, attn_low.reshape(row_count, model), wide_tokens, vectors,
-        ),
-        "attention_backward",
-    )
-
     own_shape = (model // data, 4 * width)
     last_pair = pltpu.VMEM((data // 2,) + own_shape, BF16)
     grad_tokens, output, own_last, own_up, own_down, sums = call(
-        functools.partial(last_kernel, sizes),
+        functools.partial(back_kernel, sizes, score_scale),
         [
             shaped(split, BF16),
             shaped(split, BF16),
@@ -997,7 +980,15 @@
             shaped((model // data, up_width), F32),
             shaped(vectors.shape, F32),
         ],
-        [flow] * 3
+        [
+            pltpu.VMEM((keys, width), F32),
+            pltpu.VMEM((keys, width), F32),
+            pltpu.VMEM((row_count, width), BF16),
+            pltpu.VMEM((blocks, row_count, 3 * width), BF16),
+            pltpu.VMEM((model, 4 * width), BF16),
+            pltpu.VMEM(vectors.shape, F32),
+        ]
+        + [flow] * 3
         + [
             pltpu.VMEM((blocks, row_count, 2 * width), BF16),
             pltpu.VMEM((row_count, 3 * width), BF16),
@@ -1018,18 +1009,14 @@
         + sems(blocks - 1) * 3,
         2,
         (
-            stack.reshape(blocks, row_count, 3 * width),
-            flat_qkv,
-            d_attn,
-            last_grads,
-            block_up,
-            block_down,
-            vectors,
-            output_part,
+            lengths, queries, key_rows, value_rows, attended, attended_low, log_total,
+            flat_proj, attn_low.reshape(row_count, model), wide_tokens, vectors,
+            flat_qkv, d_attn, block_up, block_down, output_part,
         ),
-        "token_grads",
-    )
-    output, grad_tokens, own_qkv, own_proj, own_up, own_down = local_call(
+        "attention_backward",
+        scalars=1,
+    )
+    output, grad_tokens, own_qkv, own_proj, own_up, own_down, grad_query, grad_value, *rows = local_call(
         unpack_kernel,
         [
             shaped((row_count, model), BF16),
@@ -1038,7 +1025,11 @@
             shaped((width, model // data), F32),
             shaped(own_up.shape, F32),
             shaped(own_down.shape, F32),
-        ],
+            shaped((width,), F32),
+            shaped((width,), F32),
+        ]
+        + [shaped((model,), F32)] * 6
+        + [shaped((up_width,), F32)],
         [],
         (
             grad_tokens.reshape(row_count, model),
@@ -1046,6 +1037,7 @@
             own_last,
             own_up,
             own_down,
+            sums,
         ),
         "unpack",
         scalars=0,
@@ -1054,18 +1046,18 @@
         output[None],
         grad_tokens[None],
         own_qkv,
-        sums[7, :width],
-        sums[7, width : 2 * width],
+        grad_query,
+        grad_value,
         own_proj,
-        sums[5, :model],
-        sums[4, :model],
-        sums[3, :model],
+        rows[5],
+        rows[4],
+        rows[3],
         own_up,
-        sums[6, :up_width],
+        rows[6],
         own_down.T,
-        sums[2, :model],
-        sums[1, :model],
-        sums[0, :model],
+        rows[2],
+        rows[1],
+        rows[0],
     )
 
 

time: 201 us -> 186 us (0.925)
  Pallas kernels: 193 us -> 185 us
  local copies, waits for them, and re-layouts: 4.45 us -> 0 us
    pallas_call x3 -> x2, Pallas kernels: 26.6 us -> 14.4 us  [local_call(): pl.pallas_call(kernel, out_shape=outs, in_specs=[pl.BlockSpec(memory_spac...]
    pallas_call x3, Pallas kernels: 167 us -> 170 us  [call(): pl.pallas_call(kernel, out_shape=outs, in_specs=[pl.BlockSpec(memory_spac...]
    slice x2 -> x0, local copies, waits for them, and re-layouts: 3.08 us -> none  [the longest x1 1.67 us: per_device(): sums[0, :model]]
where the time goes in v2:
time: 186 us
  Pallas kernels  185 us (99%)
    pallas_call x3, Pallas kernels, call(): pl.pallas_call(kernel, out_shape=outs, in_specs=[pl.BlockSpec(memory_spac...  170 us
    pallas_call x2, Pallas kernels, local_call(): pl.pallas_call(kernel, out_shape=outs, in_specs=[pl.BlockSpec(memory_spac...  14.4 us

profile of v2, /device:TPU:0, one launch (start us, length us, event | category | flops | bytes accessed | tf_op | source)
XLA Modules:
  0.0 186.3 jit_solution(17617096176030215283)
XLA Ops:
  1.3 21.0 %gather_inputs.1 = (bf16[2,512,768]{2,1,0:T(8,128)(2,1)}, bf16[3,768,192]{2,1,0:T(8,128)(2,1)}, bf16[4,192,192]{2,1,0:T(8,128)(2,1)}) custom-call(bf16[512,768]{1,0:T(8,128)(2,1)} %bitcast.12, bf16[3,192,192]{2,1,0:T(8,128)(2,1)} %qkv.1, bf16[192,192]{1,0:T(8,128)(2,1)} %proj.1), custom_call_target="tpu_custom_call" | custom-call | tf_op jit(solution)/shard_map/gather_inputs/pallas_call | solution.py:116
  22.3 10.1 %attention_forward.1 = (bf16[512,192]{1,0:T(8,128)(2,1)}, bf16[1024,192]{1,0:T(8,128)(2,1)}, bf16[1024,192]{1,0:T(8,128)(2,1)}, f32[512,192]{1,0:T(8,128)}, bf16...) custom-call(s32[1]{0:T(128)S(6)} %copy.31.length_ref, ...), custom_call_target="tpu_custom_call" | custom-call | tf_op jit(solution)/shard_map/attention_forward/pallas_call | solution.py:841
  32.5 89.4 %norms_and_hidden.1 = (bf16[2,8,32,768]{3,2,1,0:T(8,128)(2,1)}, f32[8,32,768]{2,1,0:T(8,128)}, bf16[8,32,768]{2,1,0:T(8,128)(2,1)}, f32[8,768]{1,0:T(8,128)}, bf...) custom-call(bf16[2,8,32,768]{3,2,1,0:T(8,128)(2,1)} %bitcast.21, bf16[2,8,32,768]{3,2,1,0:T(8,128)(2,1)} %bitcast.14, ...), custom_call_target="tpu_custom_call" | custom-call | tf_op jit(solution)/shard_map/norms_and_hidden/pallas_call | solution.py:116
  121.8 60.0 %attention_backward.1 = (bf16[2,8,32,768]{3,2,1,0:T(8,128)(2,1)}, bf16[2,8,32,768]{3,2,1,0:T(8,128)(2,1)}, f32[192,768]{1,0:T(8,128)}, f32[192,768]{1,0:T(8,128)}, f32[192,768]{1,0:T(8,128)}, /*index=5*/f32[8,768]{1,0:T(8,128)}) custom-call(s32[1]{0:T(128)S(6)} %copy.31.length_ref, bf16[512,192]{1,0:T(8,128)(2,1)} %get-tuple-element.58.q_ref, ...), custom_call_target="tpu_custom_call" | custom-call | tf_op jit(solution)/shard_map/attention_backward/pallas_call | solution.py:116
  181.8 4.3 %unpack.1 = (bf16[512,768]{1,0:T(8,128)(2,1)}, f32[512,768]{1,0:T(8,128)}, f32[3,192,192]{2,1,0:T(8,128)}, f32[192,192]{1,0:T(8,128)}, f32[192,768]{1,0:T(8,128)...) custom-call(bf16[512,768]{1,0:T(8,128)(2,1)} %bitcast.19, ...), custom_call_target="tpu_custom_call" | custom-call | tf_op jit(solution)/shard_map/unpack/pallas_call | solution.py:841

commit v3 on v2

--- a/solution.py
+++ b/solution.py
@@ -394,83 +394,114 @@
     return lax.rem(step, 2), lax.div(step, 2) * group
 
 
-def gather_kernel(sizes, tokens, qkv, proj, wide_tokens, wide_qkv, wide_proj, *sem):
-    data, blocks, ranks = sizes["dp"], sizes["ctx"], sizes["tensor"]
+def front_kernel(
+    sizes, score_scale, given_count, length_ref, tokens, qkv, proj, cotangent, up, down, *refs
+):
+    data, blocks, size = sizes["dp"], sizes["ctx"], sizes["tensor"]
+    given, refs = refs[:given_count], refs[given_count:]
+    q_ref, k_ref, v_ref, out_ref, low_ref, log_ref, proj_ref, flat_ref, wide_tokens = refs[:9]
+    middle_outs, refs = refs[9:15], refs[15:]
+    wide_qkv, wide_proj, fixed, part = refs[:4]
+    middle_scratch, sem = refs[4:31], refs[31:]
+    wide_up, wide_down, slots = middle_scratch[0], middle_scratch[1], middle_scratch[15]
+    sem_tokens, sem_qkv, sem_proj = sem[0:4], sem[4:10], sem[10:16]
+    sem_middle = sem[16:]
     me, rank = lax.axis_index("ctx"), lax.axis_index("tensor")
+    mine = lax.axis_index("dp")
     mate = rank + 1 - 2 * lax.rem(rank, 2)
     peers = peers_of("ctx", blocks)
     piece = qkv.shape[1]
-    rows = tokens.shape[0] // 2 // PIECES
-
-    def span(parity, index):
-        return pl.ds(pl.multiple_of((parity * PIECES + index) * rows, rows), rows)
-
-    own_half = lax.rem(rank, 2)
-    greet([peers, [(mate, {"tensor": mate})], pair_group(data)])
+    rows, model = tokens.shape
+    width = q_ref.shape[1]
+    count = rows // 2 // PIECES
+
+    def span(index):
+        return pl.ds(pl.multiple_of((lax.rem(rank, 2) * PIECES + index) * count, count), count)
+
+    greet_line(size, [peers, pair_group(data)])
     across = []
     for index in range(PIECES):
         for step, (_, where) in enumerate(peers):
-            here = span(own_half, index)
             across.append(
-                remote(tokens.at[here], wide_tokens.at[me, here], sem[0].at[step, index], sem[1].at[step, index], where)
+                remote(
+                    tokens.at[span(index)],
+                    wide_tokens.at[me, span(index)],
+                    sem_tokens[0].at[step, index],
+                    sem_tokens[1].at[step, index],
+                    where,
+                )
             )
             across[-1].start()
     place_qkv = lambda index: wide_qkv.at[:, part_rows(index, piece)]
     place_proj = lambda index: wide_proj.at[index]
-    copies = gather_start(data, qkv, place_qkv, sem[4:10])
-    projs = gather_start(data, proj, place_proj, sem[10:16])
-    mine = lax.axis_index("dp")
+    place_up = lambda index: wide_up.at[part_rows(index, piece)]
+    place_down = lambda index: wide_down.at[part_rows(index, piece)]
+    copies = gather_start(data, qkv, place_qkv, sem_qkv)
+    projs = gather_start(data, proj, place_proj, sem_proj)
+    ups = gather_start(data, up, place_up, sem_middle[12:18])
+    downs = gather_start(data, down, place_down, sem_middle[18:24])
     wide_qkv[:, part_rows(mine, piece)] = qkv[...]
     wide_proj[mine] = proj[...]
     wide_tokens[me] = tokens[...]
+    wide_up[part_rows(mine, piece)] = up[...]
+    wide_down[part_rows(mine, piece)] = down[...]
+    for index, vector in enumerate(given):
+        fixed[index : index + 1, : vector.shape[0]] = vector[...].reshape(1, -1)
     passed = []
-    for index in range(PIECES):
+
+    def forward_piece(index):
         for step in range(len(peers)):
             origin = lax.rem(me + blocks - step - 1, blocks)
             across[index * len(peers) + step].wait_recv()
-            here = span(own_half, index)
-            place = wide_tokens.at[origin, here]
+            place = wide_tokens.at[origin, span(index)]
             passed.append(
-                remote(place, place, sem[2].at[step, index], sem[3].at[step, index], {"tensor": mate})
+                remote(place, place, sem_tokens[2].at[step, index], sem_tokens[3].at[step, index], {"tensor": mate})
             )
             passed[-1].start()
-    passing = gather_pass(data, copies, place_qkv, sem[4:10])
-    passing += gather_pass(data, projs, place_proj, sem[10:16])
-    for copy in across:
-        copy.wait_send()
-    wait_all(passed)
-    wait_all(passing)
-
-
-def forward_kernel(
-    sizes, score_scale, length_ref, tokens, wide_tokens, wide_qkv, wide_proj, *refs
-):
-    given, (q_ref, k_ref, v_ref, out_ref, low_ref, log_ref, part_ref, proj_ref, flat_ref, fixed) = refs[:-10], refs[-10:]
-    length = length_ref[0]
-    for index, vector in enumerate(given):
-        fixed[index : index + 1, : vector.shape[0]] = vector[...].reshape(1, -1)
-    rows, width = q_ref.shape
-    keys = k_ref.shape[0]
-    block = math.gcd(rows, ROW_BLOCK)
-    column = wide_proj.shape[2]
-    for index in range(sizes["dp"]):
-        proj_ref[:, index * column : (index + 1) * column] = wide_proj[index]
-    for slot, index in enumerate((1, 2, 0)):
-        flat_ref[:, slot * width : (slot + 1) * width] = wide_qkv[index]
-
-    @pl.loop(0, keys // block)
-    def _(step):
-        here = part_rows(step, block)
-        found = wide_tokens[here]
+
+    for index in range(PIECES - 1):
+        forward_piece(index)
+    wait_all(gather_pass(data, copies, place_qkv, sem_qkv))
+    forward_piece(PIECES - 1)
+    block = math.gcd(rows // 2, ROW_BLOCK)
+
+    def project(origin, step):
+        there = part_rows(step, block)
+        here = pl.ds(pl.multiple_of(origin * rows + step * block, block), block)
+        found = wide_tokens[origin, there]
         k_ref[here] = matmul(found, wide_qkv[1]).astype(BF16)
         v_ref[here] = (matmul(found, wide_qkv[2]) + fixed[8:9, :width]).astype(BF16)
-
-    hidden_keys = lax.broadcasted_iota(jnp.int32, (block, keys), 1) >= length
 
     @pl.loop(0, rows // block)
     def _(step):
         here = part_rows(step, block)
         q_ref[here] = (matmul(tokens[here], wide_qkv[0]) + fixed[7:8, :width]).astype(BF16)
+        project(me, step)
+
+    for slot, index in enumerate((1, 2, 0)):
+        flat_ref[:, slot * width : (slot + 1) * width] = wide_qkv[index]
+    wait_all(gather_pass(data, projs, place_proj, sem_proj))
+    column = wide_proj.shape[2]
+    for index in range(data):
+        proj_ref[:, index * column : (index + 1) * column] = wide_proj[index]
+    for copy in across:
+        copy.wait_send()
+    wait_all(passed)
+
+    @pl.loop(0, (blocks - 1) * (rows // block))
+    def _(step):
+        other = lax.rem(me + 1 + lax.div(step, rows // block), blocks)
+        project(other, lax.rem(step, rows // block))
+
+    length = length_ref[0]
+    keys = k_ref.shape[0]
+    hidden_keys = lax.broadcasted_iota(jnp.int32, (block, keys), 1) >= length
+    chunks, chunk = part.shape[1:3]
+    group = block // chunk
+
+    @pl.loop(0, rows // block)
+    def _(step):
+        here = part_rows(step, block)
         for head in range(width // HD):
             lanes = slice(head * HD, (head + 1) * HD)
             scores = matmul_last(q_ref[here, lanes], k_ref[:, lanes]) * score_scale
@@ -482,7 +513,14 @@
             out_ref[here, lanes] = attended
             low_ref[here, lanes] = attended.astype(BF16)
             log_ref[here, head : head + 1] = top + jnp.log(total)
-        part_ref[here] = matmul(low_ref[here], proj_ref[...]).astype(BF16)
+        flow, begin = lax.div(step * group, chunks), lax.rem(step * group, chunks)
+        result = matmul(low_ref[here], proj_ref[...]).astype(BF16)
+        part[flow, pl.ds(begin, group)] = result.reshape(group, chunk, model)
+        line_start_block(size, part, slots, sem_middle[0:4], flow, begin, group)
+
+    passing = gather_pass(data, ups, place_up, sem_middle[12:18])
+    passing += gather_pass(data, downs, place_down, sem_middle[18:24])
+    middle_steps(sizes, passing, part, tokens, cotangent, fixed, up, *middle_outs, *middle_scratch, *sem_middle)
 
 
 def near_start(size, grads, chip, sem):
@@ -530,8 +568,8 @@
     )
 
 
-def middle_kernel(
-    sizes, part, tokens, cotangent, fixed, up, down,
+def middle_steps(
+    sizes, passing, part, tokens, cotangent, fixed, up,
     attn_low, attn_ref, output_ref, vector_ref, block_up, block_down,
     wide_up, wide_down, low, normed_ref, inverse_ref, out_ref, pre, hidden,
     part_two, back_ref, second_low, d_pre, part_three, grads_up, grads_down,
@@ -548,32 +586,19 @@
     line_one, line_two, line_three = sem[0:4], sem[4:8], sem[8:12]
     sem_up, sem_down = sem[12:18], sem[18:24]
     sem_a, sem_b = sem[24:28], sem[28:32]
-    greet_line(size, [pair_group(data)])
-    line_start(size, part, slots, line_one)
-    place_up = lambda index: wide_up.at[part_rows(index, piece)]
-    place_down = lambda index: wide_down.at[part_rows(index, piece)]
-    ups = gather_start(data, up, place_up, sem_up)
-    downs = gather_start(data, down, place_down, sem_down)
-    wide_up[part_rows(mine, piece)] = up[...]
-    wide_down[part_rows(mine, piece)] = down[...]
     vector_ref[...] = jnp.zeros_like(vector_ref)
 
     def first_finish(flow, k, total):
-        first_sum = tokens[flow, k].astype(F32) + total + fixed[0:1, :model]
+        here = pl.ds(pl.multiple_of((flow * chunks + k) * chunk, chunk), chunk)
+        first_sum = tokens[here].astype(F32) + total + fixed[0:1, :model]
         first_out, normed, inverse = layer_norm(first_sum, fixed[1:2, :model], fixed[2:3, :model])
         out_ref[k] = first_out
         normed_ref[k] = normed
         inverse_ref[k] = inverse
         return first_out.astype(BF16)
 
-    passed = []
-
-    def hand_over():
-        passed.extend(gather_pass(data, ups, place_up, sem_up))
-        passed.extend(gather_pass(data, downs, place_down, sem_down))
-
-    line_run(size, part, slots, sums, low, line_one, first_finish, [(LAG * size, hand_over)])
-    wait_all(passed)
+    line_run(size, part, slots, sums, low, line_one, first_finish)
+    wait_all(passing)
 
     @pl.loop(0, steps)
     def _(step):
@@ -889,21 +914,14 @@
         proj_bias, first_gain, first_shift, down_bias, second_gain, second_shift, up_bias, query_bias, value_bias
     )
 
-    wide_tokens, wide_qkv, wide_proj = call(
-        functools.partial(gather_kernel, sizes),
-        [
-            shaped((blocks, row_count, model), BF16),
-            shaped((3, model, width), BF16),
-            shaped((data,) + proj_weight.shape, BF16),
-        ],
-        [DMA((blocks - 1, PIECES))] * 4 + pair_sems(data) * 2,
-        0,
-        (rows_in, qkv_weight, proj_weight),
-        "gather_inputs",
-    )
-    wide_tokens = wide_tokens.reshape(keys, model)
-    queries, key_rows, value_rows, attended, attended_low, log_total, attn_part, flat_proj, flat_qkv, fixed = local_call(
-        functools.partial(forward_kernel, sizes, score_scale),
+    up_shape = (model, up_width)
+    pair_slots = pltpu.VMEM((data // 2, model // data, up_width), BF16)
+    pair_moves = sems(data // 2) + sems(max(1, data // 2 - 1))
+    (
+        queries, key_rows, value_rows, attended, attended_low, log_total, flat_proj, flat_qkv, wide_tokens,
+        attn_low, d_attn, output_part, vectors, block_up, block_down,
+    ) = call(
+        functools.partial(front_kernel, sizes, score_scale, len(given)),
         [
             shaped((row_count, width), BF16),
             shaped((keys, width), BF16),
@@ -911,22 +929,9 @@
             shaped((row_count, width), F32),
             shaped((row_count, width), BF16),
             shaped((row_count, width // HD), F32),
-            shaped((row_count, model), BF16),
             shaped((width, model), BF16),
             shaped((model, 3 * width), BF16),
-            shaped((16, vector_width), F32),
-        ],
-        [],
-        (lengths, rows_in, wide_tokens, wide_qkv, wide_proj) + given,
-        "attention_forward",
-    )
-
-    up_shape = (model, up_width)
-    pair_slots = pltpu.VMEM((data // 2, model // data, up_width), BF16)
-    pair_moves = sems(data // 2) + sems(max(1, data // 2 - 1))
-    attn_low, d_attn, output_part, vectors, block_up, block_down = call(
-        functools.partial(middle_kernel, sizes),
-        [
+            shaped((blocks, row_count, model), BF16),
             shaped(split, BF16),
             local,
             shaped(split[1:], BF16),
@@ -935,6 +940,12 @@
             shaped((model // data, up_width), BF16),
         ],
         [
+            pltpu.VMEM((3, model, width), BF16),
+            pltpu.VMEM((data,) + proj_weight.shape, BF16),
+            pltpu.VMEM((16, vector_width), F32),
+            flow,
+        ]
+        + [
             pltpu.VMEM(up_shape, BF16),
             pltpu.VMEM(up_shape, BF16),
             flow,
@@ -953,20 +964,17 @@
         ]
         + [flow] * 6
         + [pair_slots] * 6
+        + [DMA((max(1, blocks - 1), PIECES))] * 4
+        + pair_sems(data) * 2
         + line * 3
         + pair_sems(data) * 2
         + pair_moves * 2,
         1,
-        (
-            attn_part.reshape(split),
-            rows_in.reshape(split),
-            cotangent[0].reshape(split),
-            fixed,
-            up_weight,
-            down_weight.T,
-        ),
-        "norms_and_hidden",
+        (lengths, rows_in, qkv_weight, proj_weight, cotangent[0].reshape(split), up_weight, down_weight.T) + given,
+        "forward_and_hidden",
+        scalars=1,
     )
+    wide_tokens = wide_tokens.reshape(keys, model)
 
     own_shape = (model // data, 4 * width)
     last_pair = pltpu.VMEM((data // 2,) + own_shape, BF16)

time: 186 us -> 181 us (0.973)
  Pallas kernels: 185 us -> 180 us
    pallas_call x2 -> x1, Pallas kernels: 14.4 us -> 4.29 us  [local_call(): pl.pallas_call(kernel, out_shape=outs, in_specs=[pl.BlockSpec(memory_spac...]
    pallas_call x3 -> x2, Pallas kernels: 170 us -> 175 us  [call(): pl.pallas_call(kernel, out_shape=outs, in_specs=[pl.BlockSpec(memory_spac...]
where the time goes in v3:
time: 181 us
  Pallas kernels  180 us (99%)
    pallas_call x2, Pallas kernels, call(): pl.pallas_call(kernel, out_shape=outs, in_specs=[pl.BlockSpec(memory_spac...  175 us
    pallas_call x1, Pallas kernels, local_call(): pl.pallas_call(kernel, out_shape=outs, in_specs=[pl.BlockSpec(memory_spac...  4.29 us

profile of v3, /device:TPU:0, one launch (start us, length us, event | category | flops | bytes accessed | tf_op | source)
XLA Modules:
  0.0 181.0 jit_solution(6236691186770467323)
XLA Ops:
  1.3 111.7 %forward_and_hidden.1 = (bf16[512,192]{1,0:T(8,128)(2,1)}, bf16[1024,192]{1,0:T(8,128)(2,1)}, bf16[1024,192]{1,0:T(8,128)(2,1)}, f32[512,192]{1,0:T(8,128)}, bf1...) custom-call(s32[1]{0:T(128)S(6)} %copy.31.length_ref, ...), custom_call_target="tpu_custom_call" | custom-call | tf_op jit(solution)/shard_map/forward_and_hidden/pallas_call | solution.py:116
  113.0 63.6 %attention_backward.1 = (bf16[2,8,32,768]{3,2,1,0:T(8,128)(2,1)}, bf16[2,8,32,768]{3,2,1,0:T(8,128)(2,1)}, f32[192,768]{1,0:T(8,128)}, f32[192,768]{1,0:T(8,128)}, f32[192,768]{1,0:T(8,128)}, /*index=5*/f32[8,768]{1,0:T(8,128)}) custom-call(s32[1]{0:T(128)S(6)} %copy.31.length_ref, bf16[512,192]{1,0:T(8,128)(2,1)} %get-tuple-element.51.q_ref, ...), custom_call_target="tpu_custom_call" | custom-call | tf_op jit(solution)/shard_map/attention_backward/pallas_call | solution.py:116
  176.6 4.3 %unpack.1 = (bf16[512,768]{1,0:T(8,128)(2,1)}, f32[512,768]{1,0:T(8,128)}, f32[3,192,192]{2,1,0:T(8,128)}, f32[192,192]{1,0:T(8,128)}, f32[192,768]{1,0:T(8,128)...) custom-call(bf16[512,768]{1,0:T(8,128)(2,1)} %bitcast.14, ...), custom_call_target="tpu_custom_call" | custom-call | tf_op jit(solution)/shard_map/unpack/pallas_call | solution.py:866

commit v4 on v3

--- a/solution.py
+++ b/solution.py
@@ -371,7 +371,7 @@
 PIECES = 4
 GROUP = 4
 ROW_BLOCK = 256
-SPREAD_LAG = 2
+SPREAD_LAG = 4
 
 
 def matmul(left, right):
@@ -732,7 +732,9 @@
     stack[:, :, 2 * width :] = jnp.zeros((sizes["ctx"], rows, width), BF16)
     heads = width // HD
     turns = rows // block * heads
-    relays = mine.shape[0] + SPREAD_LAG * (size - 1)
+    relays_all = mine.shape[0] + SPREAD_LAG * (size - 1)
+    relays_sent = mine.shape[0] + SPREAD_LAG * (size - 2)
+    relays = relays_sent - 2
 
     @pl.loop(0, rows // block)
     def _(step):
@@ -824,12 +826,14 @@
     def finish(flow, k, total):
         return (total + d_attn[k]).astype(BF16)
 
+    spread_steps(size, mine, output_ref, spread, relays, relays_sent)
     for step in range(2):
         send_group(step)
     between = [(1, go_far)]
     between += [(LAG + 2 * step - 3, functools.partial(send_group, step)) for step in range(2, steps)]
     between += [(max(LAG * size, LAG + 2 * steps), go_across)]
     line_run(size, part, slots, sums, full, line, finish, between)
+    spread_steps(size, mine, output_ref, spread, relays_sent, relays_all)
     spread_end(size, mine, output_ref, spread)
     for copies in moving_keys:
         for copy in copies:

time: 181 us -> 174 us (0.961)
  Pallas kernels: 180 us -> 172 us
    pallas_call x2, Pallas kernels: 175 us -> 168 us  [call(): pl.pallas_call(kernel, out_shape=outs, in_specs=[pl.BlockSpec(memory_spac...]
where the time goes in v4:
time: 174 us; the launch traced here: 173 us
  Pallas kernels  172 us (99%)
    pallas_call x2, Pallas kernels, call(): pl.pallas_call(kernel, out_shape=outs, in_specs=[pl.BlockSpec(memory_spac...  168 us
    pallas_call x1, Pallas kernels, local_call(): pl.pallas_call(kernel, out_shape=outs, in_specs=[pl.BlockSpec(memory_spac...  4.29 us

profile of v4, /device:TPU:0, one launch (start us, length us, event | category | flops | bytes accessed | tf_op | source)
XLA Modules:
  0.0 173.3 jit_solution(16029936015818682871)
XLA Ops:
  1.3 111.7 %forward_and_hidden.1 = (bf16[512,192]{1,0:T(8,128)(2,1)}, bf16[1024,192]{1,0:T(8,128)(2,1)}, bf16[1024,192]{1,0:T(8,128)(2,1)}, f32[512,192]{1,0:T(8,128)}, bf1...) custom-call(s32[1]{0:T(128)S(6)} %copy.31.length_ref, ...), custom_call_target="tpu_custom_call" | custom-call | tf_op jit(solution)/shard_map/forward_and_hidden/pallas_call | solution.py:116
  113.0 55.9 %attention_backward.1 = (bf16[2,8,32,768]{3,2,1,0:T(8,128)(2,1)}, bf16[2,8,32,768]{3,2,1,0:T(8,128)(2,1)}, f32[192,768]{1,0:T(8,128)}, f32[192,768]{1,0:T(8,128)}, f32[192,768]{1,0:T(8,128)}, /*index=5*/f32[8,768]{1,0:T(8,128)}) custom-call(s32[1]{0:T(128)S(6)} %copy.31.length_ref, bf16[512,192]{1,0:T(8,128)(2,1)} %get-tuple-element.51.q_ref, ...), custom_call_target="tpu_custom_call" | custom-call | tf_op jit(solution)/shard_map/attention_backward/pallas_call | solution.py:116
  168.9 4.3 %unpack.1 = (bf16[512,768]{1,0:T(8,128)(2,1)}, f32[512,768]{1,0:T(8,128)}, f32[3,192,192]{2,1,0:T(8,128)}, f32[192,192]{1,0:T(8,128)}, f32[192,768]{1,0:T(8,128)...) custom-call(bf16[512,768]{1,0:T(8,128)(2,1)} %bitcast.14, ...), custom_call_target="tpu_custom_call" | custom-call | tf_op jit(solution)/shard_map/unpack/pallas_call | solution.py:870
